TPU v7x, 128 devices: a whole 4x4x4 slice. The times are simulated.
128 devices in a mesh: gx: 16 (over z, y), gy: 8 (over x, core).
Axes of the slice: x: 4, y: 4, z: 4, core: 2. Of those that a mesh axis runs over, the one named last changes fastest.
Arguments:
- velocity: float32 [3, 16, 2048, 2048], P(None, None, 'gx', 'gy'), may hold values from -6 to 6
- metric_x: float32 [2048], replicated, may hold values from 0.5 to 2
- metric_y: float32 [2048], replicated, may hold values from 0.5 to 2
- marker_force: float32 [3, 262144], P(None, ('gx', 'gy')), may hold values from -24 to 24
- marker_frac: float32 [3, 262144], P(None, ('gx', 'gy')), may hold values from 0 to 1
- marker_cell_x: int32 [262144], P(('gx', 'gy')), may hold values from 0 to 127
- marker_cell_y: int32 [262144], P(('gx', 'gy')), may hold values from 0 to 255
- marker_cell_z: int32 [262144], P(('gx', 'gy')), may hold values from 0 to 15
- send_counts: int32 [128, 128], P(('gx', 'gy')), may hold values from 0 to 32, as said below
Outputs:
- ddx: float32 [3, 16, 2048, 2048], P(None, None, 'gx', 'gy')
- ddy: float32 [3, 16, 2048, 2048], P(None, None, 'gx', 'gy')
Inputs may be any that keep to these rules, and one draw needn't show every extreme that they name: `send_counts`: row s lists, block by block in gx+gy order, how many of source device s's markers each grid block owns; the markers of a device come in that block order; each row sums to 2048; in every draw some block owns 32 markers of every source device.
All inputs are finite; a program needn't handle non-finite values.
Results may differ from a plain program's by a relative error of at most 0.00035.
Values sent between devices are 32-bit elements; how exact they have to be, the bound alone decides.
A program may use at most 640 MiB of HBM per device.

v0:
```python
import jax
import jax.numpy as jnp
from jax import lax
from jax.sharding import PartitionSpec as P

CAP = 32


section_weight = 0.5


def with_halo(cells, sides, width):
    for axis, dim in sides:
        count = lax.axis_size(axis)
        head = lax.slice_in_dim(cells, 0, width, axis=dim)
        tail = lax.slice_in_dim(cells, cells.shape[dim] - width, cells.shape[dim], axis=dim)
        cells = jnp.concatenate(
            [
                lax.ppermute(tail, axis, [(i, (i + 1) % count) for i in range(count)]),
                cells,
                lax.ppermute(head, axis, [((i + 1) % count, i) for i in range(count)]),
            ],
            axis=dim,
        )
    return cells


def kernel_weights(frac):
    root = jnp.sqrt(1.0 + 4.0 * frac - 4.0 * frac * frac)
    return (
        (3.0 - 2.0 * frac - root) / 8.0,
        (3.0 - 2.0 * frac + root) / 8.0,
        (1.0 + 2.0 * frac + root) / 8.0,
        (1.0 + 2.0 * frac - root) / 8.0,
    )


def weight_table(positions, weights, width):
    columns = jnp.arange(width, dtype=jnp.int32)
    table = jnp.zeros((positions[0].shape[0], width), jnp.float32)
    for offset in range(4):
        table = table + jnp.where(
            columns[None, :] == positions[offset][:, None], weights[offset][:, None], 0.0
        )
    return table


def spread_block(force, frac, codes, planes, rows, cols):
    cell_z = codes % planes
    rest = codes // planes
    cell_y = rest % cols
    cell_x = rest // cols
    table_x = weight_table(
        [cell_x + 1 + offset for offset in range(4)], kernel_weights(frac[0]), rows + 4
    )
    table_y = weight_table(
        [cell_y + 1 + offset for offset in range(4)], kernel_weights(frac[1]), cols + 4
    )
    table_z = weight_table(
        [(cell_z - 1 + offset) % planes for offset in range(4)], kernel_weights(frac[2]), planes
    )
    scaled = force[:, None, None, :] * table_z.T[None, :, None, :] * table_x.T[None, None, :, :]
    return jnp.einsum("czxb,by->czxy", scaled, table_y, precision=lax.Precision.HIGHEST)


def fold_rims(padded, rows, cols):
    inner = padded[:, :, 4 : rows + 4, :]
    inner = inner.at[:, :, 0:2, :].add(padded[:, :, 0:2, :])
    inner = inner.at[:, :, rows - 1, :].add(padded[:, :, rows + 7, :])
    folded = inner[:, :, :, 4 : cols + 4]
    folded = folded.at[:, :, :, 0:2].add(inner[:, :, :, 0:2])
    folded = folded.at[:, :, :, cols - 1].add(inner[:, :, :, cols + 7])
    return folded


def band_inverse(length):
    lower = jnp.full((length,), 1.0 / 3.0, jnp.float32).at[0].set(0.0)
    upper = jnp.full((length,), 1.0 / 3.0, jnp.float32).at[length - 1].set(0.0)
    middle = jnp.ones((length,), jnp.float32)
    inverse = lax.linalg.tridiagonal_solve(lower, middle, upper, jnp.eye(length, dtype=jnp.float32))
    return (inverse, (lower, middle, upper))


def solve_lines(rhs, inverse, axis):
    if axis == 2:
        return jnp.einsum("ij,czjy->cziy", inverse, rhs, precision=lax.Precision.HIGHEST)
    return jnp.einsum("ij,czxj->czxi", inverse, rhs, precision=lax.Precision.HIGHEST)


def attach(partial_sol, left_last, right_first, inverse, axis):
    length = inverse.shape[0]
    corner = inverse[0, 0]
    divisor = 1.0 - corner * corner / 9.0
    if axis == 2:
        first = partial_sol[:, :, 0, :]
        last = partial_sol[:, :, length - 1, :]
    else:
        first = partial_sol[:, :, :, 0]
        last = partial_sol[:, :, :, length - 1]
    from_left = (left_last - corner / 3.0 * first) / divisor
    from_right = (right_first - corner / 3.0 * last) / divisor
    if axis == 2:
        return (
            partial_sol
            - (
                from_left[:, :, None, :] * inverse[:, 0][None, None, :, None]
                + from_right[:, :, None, :] * inverse[:, length - 1][None, None, :, None]
            )
            / 3.0
        )
    return (
        partial_sol
        - (
            from_left[:, :, :, None] * inverse[:, 0]
            + from_right[:, :, :, None] * inverse[:, length - 1]
        )
        / 3.0
    )


def solve_both(padded, local_x, local_y, solvers):
    rows, cols = (padded.shape[2] - 4, padded.shape[3] - 4)
    inverse_x, bands_x, inverse_y, bands_y = solvers
    rhs_x = 7.0 / 9.0 * (
        padded[:, :, 3 : rows + 3, 2 : cols + 2] - padded[:, :, 1 : rows + 1, 2 : cols + 2]
    ) + 1.0 / 36.0 * (padded[:, :, 4 : rows + 4, 2 : cols + 2] - padded[:, :, 0:rows, 2 : cols + 2])
    rhs_y = 7.0 / 9.0 * (
        padded[:, :, 2 : rows + 2, 3 : cols + 3] - padded[:, :, 2 : rows + 2, 1 : cols + 1]
    ) + 1.0 / 36.0 * (padded[:, :, 2 : rows + 2, 4 : cols + 4] - padded[:, :, 2 : rows + 2, 0:cols])
    part_x = solve_lines(rhs_x, inverse_x, 2)
    ends_x = jnp.stack((part_x[:, :, 0, :], part_x[:, :, rows - 1, :]), axis=2)
    near_x = with_halo(ends_x, (("gx", 2),), 1)
    grad_x = (
        attach(part_x, near_x[:, :, 0, :], near_x[:, :, 3, :], inverse_x, 2)
        * local_x[None, None, :, None]
    )
    part_y = solve_lines(rhs_y, inverse_y, 3)
    ends_y = jnp.stack((part_y[:, :, :, 0], part_y[:, :, :, cols - 1]), axis=2)
    near_y = with_halo(ends_y, (("gy", 2),), 1)
    grad_y = (
        attach(part_y, near_y[:, :, 0, :], near_y[:, :, 3, :], inverse_y, 3)
        * local_y[None, None, None, :]
    )
    return (grad_x, grad_y)


def derivatives(field, local_x, local_y, solvers):
    padded = with_halo(field, (("gx", 2), ("gy", 3)), 2)
    return solve_both(padded, local_x, local_y, solvers)


def local(
    velocity,
    metric_x,
    metric_y,
    marker_force,
    marker_frac,
    marker_cell_x,
    marker_cell_y,
    marker_cell_z,
    send_counts,
):
    planes, rows, cols = (velocity.shape[1], velocity.shape[2], velocity.shape[3])
    inverse_x, bands_x = band_inverse(rows)
    inverse_y, bands_y = band_inverse(cols)
    solvers = (inverse_x, bands_x, inverse_y, bands_y)
    index_x = (
        lax.axis_index("gx") * rows - 2 + jnp.arange(rows + 4, dtype=jnp.int32)
    ) % metric_x.shape[0]
    index_y = (
        lax.axis_index("gy") * cols - 2 + jnp.arange(cols + 4, dtype=jnp.int32)
    ) % metric_y.shape[0]
    margin_x = jnp.take(metric_x, index_x)
    margin_y = jnp.take(metric_y, index_y)
    local_x = margin_x[2 : rows + 2]
    local_y = margin_y[2 : cols + 2]
    counts = send_counts[0]
    starts = jnp.cumsum(counts) - counts
    slots = jnp.arange(CAP, dtype=jnp.int32)
    live = (slots[None, :] < counts[:, None]).reshape(-1)
    picked = jnp.minimum(starts[:, None] + slots[None, :], marker_force.shape[1] - 1).reshape(-1)
    codes = (marker_cell_x * cols + marker_cell_y) * planes + marker_cell_z
    payload = jnp.concatenate((marker_force, marker_frac), axis=0)
    outgoing = jnp.where(live[None, :], jnp.take(payload, picked, axis=1), 0.0)
    out_codes = jnp.where(live, jnp.take(codes, picked), 0)[None, :]
    incoming, got_codes = (
        lax.all_to_all(outgoing, ("gx", "gy"), split_axis=1, concat_axis=1, tiled=True),
        lax.all_to_all(out_codes, ("gx", "gy"), split_axis=1, concat_axis=1, tiled=True),
    )
    in_codes = got_codes.reshape(-1)
    total = incoming.shape[1]
    block = min(512, total)
    turns = total // block

    def add_block(turn, grid):
        start = turn * block
        piece = lax.dynamic_slice_in_dim(incoming, start, block, 1)
        piece_codes = lax.dynamic_slice_in_dim(in_codes, start, block, 0)
        return grid + spread_block(piece[0:3], piece[3:6], piece_codes, planes, rows, cols)

    spread = lax.fori_loop(
        0, turns, add_block, jnp.zeros((3, planes, rows + 4, cols + 4), jnp.float32)
    )
    padded = with_halo(spread, (("gx", 2), ("gy", 3)), 2)
    density = (
        fold_rims(padded, rows, cols) * local_x[None, None, :, None] * local_y[None, None, None, :]
    )
    forced = velocity + section_weight * density
    return derivatives(forced, local_x, local_y, solvers)


def solution(mesh):
    placed = (
        P(None, None, "gx", "gy"),
        P(),
        P(),
        P(None, ("gx", "gy")),
        P(None, ("gx", "gy")),
        P(("gx", "gy")),
        P(("gx", "gy")),
        P(("gx", "gy")),
        P(("gx", "gy"), None),
    )
    return jax.shard_map(
        local,
        mesh=mesh,
        in_specs=placed,
        out_specs=(P(None, None, "gx", "gy"), P(None, None, "gx", "gy")),
        check_vma=False,
    )
```

profile of v0, /device:TPU:1, one launch (start us, length us, event | category | flops | bytes accessed | tf_op | source)
XLA Modules:
  0.0 838.9 jit_solution(11724101866069879462)
XLA Ops:
  3.3 23.0 %gather_fusion.1 = s32[4096]{0:T(1024)S(1)} fusion(s32[2048]{0:T(1024)S(1)} %multiply_add_fusion.4, s32[4096]{0:T(1024)S(1)} %broadcast_clamp_fusion), kind=kCustom, calls=%fused_computation.1 | custom fusion | bytes 49152 | tf_op jit(solution)/shard_map/jit(_take)/gather | solution.py:185
  27.2 11.5 %all-to-all-start.1 = ((s32[1,128,32]{2,0,1:T(1,128)}), s32[1,128,32]{2,0,1:T(1,128)S(1)}, u32[]{:S(2)}, u32[]{:S(2)}) async-start(s32[1,128,32]{2,0,1:T(1,128)} %bitcast.395), calls=%async_computation.1 | async-start | bytes 131072 | tf_op jit(solution)/shard_map/all_to_all | solution.py:188
  38.8 14.9 %while.97 = (s32[]{:T(128)}, f32[]{:T(128)}, f32[256]{0:T(256)S(1)}, f32[7,32]{1,0:T(8,128)S(1)}, f32[7,32,256]{2,1,0:T(8,128)S(1)}, /*index=5*/f32[7,32,256]{2,...) while((s32[]{:T(128)}, f32[]{:T(128)}, ...), condition=%wide.region_8.9_spmd, body=%wide.region_7.8_spmd.sunk | while | flops 24705 | bytes 267869 | solution.py:80
  66.0 152.7 %while.98 = (s32[]{:T(128)}, f32[256]{0:T(256)S(1)}, f32[7,32,256]{2,1,0:T(8,128)S(1)}, f32[7,32,256]{2,1,0:T(8,128)S(1)}, f32[7,32]{1,0:T(8,128)S(1)}, /*index=...) while((s32[]{:T(128)}, f32[256]{0:T(256)S(1)}, ...), condition=%wide.region_10.11_spmd, body=%wide.region_9.10_spmd.sunk | while | flops 16418 | bytes 266713 | solution.py:80
  67.7 20.0 %multiply_subtract_fusion.125 = (f32[256]{0:T(256)S(1)}, f32[256]{0:T(256)S(1)}, f32[256]{0:T(256)S(1)}, f32[256]{0:T(256)S(1)}, f32[256]{0:T(256)S(1)}, /*index...) fusion(f32[256]{0:T(256)S(1)} %bitcast.2331, ...), kind=kLoop, calls=%fused_computation.330.clone.1 | loop fusion | flops 16384 | bytes 66688 | tf_op jit(solution)/shard_map/while/body/eval_jaxpr/sub | solution.py:80
  89.5 20.0 %multiply_subtract_fusion.125 = (f32[256]{0:T(256)S(1)}, f32[256]{0:T(256)S(1)}, f32[256]{0:T(256)S(1)}, f32[256]{0:T(256)S(1)}, f32[256]{0:T(256)S(1)}, /*index...) fusion(f32[256]{0:T(256)S(1)} %bitcast.2331, ...), kind=kLoop, calls=%fused_computation.330.clone.1 | loop fusion | flops 16384 | bytes 66688 | tf_op jit(solution)/shard_map/while/body/eval_jaxpr/sub | solution.py:80
  111.3 20.0 %multiply_subtract_fusion.125 = (f32[256]{0:T(256)S(1)}, f32[256]{0:T(256)S(1)}, f32[256]{0:T(256)S(1)}, f32[256]{0:T(256)S(1)}, f32[256]{0:T(256)S(1)}, /*index...) fusion(f32[256]{0:T(256)S(1)} %bitcast.2331, ...), kind=kLoop, calls=%fused_computation.330.clone.1 | loop fusion | flops 16384 | bytes 66688 | tf_op jit(solution)/shard_map/while/body/eval_jaxpr/sub | solution.py:80
  133.1 20.0 %multiply_subtract_fusion.125 = (f32[256]{0:T(256)S(1)}, f32[256]{0:T(256)S(1)}, f32[256]{0:T(256)S(1)}, f32[256]{0:T(256)S(1)}, f32[256]{0:T(256)S(1)}, /*index...) fusion(f32[256]{0:T(256)S(1)} %bitcast.2331, ...), kind=kLoop, calls=%fused_computation.330.clone.1 | loop fusion | flops 16384 | bytes 66688 | tf_op jit(solution)/shard_map/while/body/eval_jaxpr/sub | solution.py:80
  154.9 20.0 %multiply_subtract_fusion.125 = (f32[256]{0:T(256)S(1)}, f32[256]{0:T(256)S(1)}, f32[256]{0:T(256)S(1)}, f32[256]{0:T(256)S(1)}, f32[256]{0:T(256)S(1)}, /*index...) fusion(f32[256]{0:T(256)S(1)} %bitcast.2331, ...), kind=kLoop, calls=%fused_computation.330.clone.1 | loop fusion | flops 16384 | bytes 66688 | tf_op jit(solution)/shard_map/while/body/eval_jaxpr/sub | solution.py:80
  176.8 20.0 %multiply_subtract_fusion.125 = (f32[256]{0:T(256)S(1)}, f32[256]{0:T(256)S(1)}, f32[256]{0:T(256)S(1)}, f32[256]{0:T(256)S(1)}, f32[256]{0:T(256)S(1)}, /*index...) fusion(f32[256]{0:T(256)S(1)} %bitcast.2331, ...), kind=kLoop, calls=%fused_computation.330.clone.1 | loop fusion | flops 16384 | bytes 66688 | tf_op jit(solution)/shard_map/while/body/eval_jaxpr/sub | solution.py:80
  198.6 20.0 %multiply_subtract_fusion.125 = (f32[256]{0:T(256)S(1)}, f32[256]{0:T(256)S(1)}, f32[256]{0:T(256)S(1)}, f32[256]{0:T(256)S(1)}, f32[256]{0:T(256)S(1)}, /*index...) fusion(f32[256]{0:T(256)S(1)} %bitcast.2331, ...), kind=kLoop, calls=%fused_computation.330.clone.1 | loop fusion | flops 16384 | bytes 66688 | tf_op jit(solution)/shard_map/while/body/eval_jaxpr/sub | solution.py:80
  219.8 10.8 %gather_fusion = f32[4096,6]{1,0:T(8,128)S(1)} fusion(f32[6,2048]{0,1:T(8,128)S(1)} %copy.49, s32[4096]{0:T(1024)S(1)} %broadcast_clamp_fusion), kind=kCustom, calls=%fused_computation | custom fusion | bytes 212992 | tf_op jit(solution)/shard_map/jit(_take)/gather | solution.py:184
  236.2 65.2 %while.96 = (s32[]{:T(128)}, f32[128]{0:T(128)S(1)}, f32[3,32,128]{2,1,0:T(8,128)S(1)}, f32[3,32,128]{2,1,0:T(8,128)S(1)}, f32[3,32]{1,0:T(4,128)S(1)}, /*index=...) while((s32[]{:T(128)}, f32[128]{0:T(128)S(1)}, ...), condition=%wide.region_6.7_spmd, body=%wide.region_5.6_spmd.sunk | while | flops 8226 | bytes 101333 | solution.py:80
  237.7 20.2 %fusion.492 = (f32[128]{0:T(128)S(1)}, f32[128]{0:T(128)S(1)}, f32[128]{0:T(128)S(1)}, f32[128]{0:T(128)S(1)}, f32[128]{0:T(128)S(1)}, /*index=5*/f32[128]{0:T(1...) fusion(f32[3,32,128]{2,1,0:T(8,128)S(1)} %get-tuple-element.227, ...), kind=kLoop, calls=%fused_computation.170.clone.1 | loop fusion | flops 8192 | bytes 33536 | tf_op jit(solution)/shard_map/while/body/eval_jaxpr/sub | solution.py:80
  259.4 20.2 %fusion.492 = (f32[128]{0:T(128)S(1)}, f32[128]{0:T(128)S(1)}, f32[128]{0:T(128)S(1)}, f32[128]{0:T(128)S(1)}, f32[128]{0:T(128)S(1)}, /*index=5*/f32[128]{0:T(1...) fusion(f32[3,32,128]{2,1,0:T(8,128)S(1)} %get-tuple-element.227, ...), kind=kLoop, calls=%fused_computation.170.clone.1 | loop fusion | flops 8192 | bytes 33536 | tf_op jit(solution)/shard_map/while/body/eval_jaxpr/sub | solution.py:80
  281.2 20.2 %fusion.492 = (f32[128]{0:T(128)S(1)}, f32[128]{0:T(128)S(1)}, f32[128]{0:T(128)S(1)}, f32[128]{0:T(128)S(1)}, f32[128]{0:T(128)S(1)}, /*index=5*/f32[128]{0:T(1...) fusion(f32[3,32,128]{2,1,0:T(8,128)S(1)} %get-tuple-element.227, ...), kind=kLoop, calls=%fused_computation.170.clone.1 | loop fusion | flops 8192 | bytes 33536 | tf_op jit(solution)/shard_map/while/body/eval_jaxpr/sub | solution.py:80
  351.2 20.3 %multiply_subtract_fusion.32 = (f32[256]{0:T(256)S(1)}, f32[256]{0:T(256)S(1)}, f32[256]{0:T(256)S(1)}, f32[256]{0:T(256)S(1)}, f32[256]{0:T(256)S(1)}, /*index=...) fusion(f32[256]{0:T(256)} %bitcast.2559, ...), kind=kLoop, calls=%fused_computation.569 | loop fusion | flops 15872 | bytes 64636 | tf_op jit(solution)/shard_map/eval_jaxpr/sub | solution.py:80
  394.8 213.5 %while.99 = (s32[]{:T(128)}, f32[3,16,132,260]{3,2,1,0:T(8,128)}, f32[6,4096]{1,0:T(8,128)S(1)}, s32[4096]{0:T(1024)S(1)}, s32[]{:T(128)}, /*index=5*/s32[]{:T(1...) while((s32[]{:T(128)}, f32[3,16,132,260]{3,2,1,0:T(8,128)}, f32[6,4096]{1,0:T(8,128)S(1)}, ...), condition=%wide.region_2.3_spmd.clone, body=%wide.region_1.0_spmd.clone.sunk | while | flops 10130318336 | bytes 14131425 | solution.py:201
  395.3 24.6 %select_add_fusion.8 = f32[3,16,132,260]{3,2,1,0:T(8,128)} fusion(f32[3,16,132,260]{3,2,1,0:T(8,128)} %get-tuple-element.2046, pred[]{:T(512)S(6)} %compare.115, f32[132,512]{1,0:T(8,128)S(1)} %select_add_fusion.6, f32[3,16,512]{2,1,0:T(8,128)S(1)} %broadcast_multiply_fusion.2, f32[512]{0:T(512)S(1)} %get-tuple-element.2026, ...), kind=kOutput, calls=%fused_computation.364.clone.1 | convolution fusion | flops 10129383424 | bytes 13563905 | tf_op jit(solution)/shard_map/while/body/eval_jaxpr/czxb,by->czxy/dot_general | solution.py:63
  420.3 26.5 %select_add_fusion.8 = f32[3,16,132,260]{3,2,1,0:T(8,128)} fusion(f32[3,16,132,260]{3,2,1,0:T(8,128)} %get-tuple-element.2046, pred[]{:T(512)S(6)} %compare.115, f32[132,512]{1,0:T(8,128)S(1)} %select_add_fusion.6, f32[3,16,512]{2,1,0:T(8,128)S(1)} %broadcast_multiply_fusion.2, f32[512]{0:T(512)S(1)} %get-tuple-element.2026, ...), kind=kOutput, calls=%fused_computation.364.clone.1 | convolution fusion | flops 10129383424 | bytes 13563905 | tf_op jit(solution)/shard_map/while/body/eval_jaxpr/czxb,by->czxy/dot_general | solution.py:63
  447.2 26.5 %select_add_fusion.8 = f32[3,16,132,260]{3,2,1,0:T(8,128)} fusion(f32[3,16,132,260]{3,2,1,0:T(8,128)} %get-tuple-element.2046, pred[]{:T(512)S(6)} %compare.115, f32[132,512]{1,0:T(8,128)S(1)} %select_add_fusion.6, f32[3,16,512]{2,1,0:T(8,128)S(1)} %broadcast_multiply_fusion.2, f32[512]{0:T(512)S(1)} %get-tuple-element.2026, ...), kind=kOutput, calls=%fused_computation.364.clone.1 | convolution fusion | flops 10129383424 | bytes 13563905 | tf_op jit(solution)/shard_map/while/body/eval_jaxpr/czxb,by->czxy/dot_general | solution.py:63
  474.1 26.5 %select_add_fusion.8 = f32[3,16,132,260]{3,2,1,0:T(8,128)} fusion(f32[3,16,132,260]{3,2,1,0:T(8,128)} %get-tuple-element.2046, pred[]{:T(512)S(6)} %compare.115, f32[132,512]{1,0:T(8,128)S(1)} %select_add_fusion.6, f32[3,16,512]{2,1,0:T(8,128)S(1)} %broadcast_multiply_fusion.2, f32[512]{0:T(512)S(1)} %get-tuple-element.2026, ...), kind=kOutput, calls=%fused_computation.364.clone.1 | convolution fusion | flops 10129383424 | bytes 13563905 | tf_op jit(solution)/shard_map/while/body/eval_jaxpr/czxb,by->czxy/dot_general | solution.py:63
  501.1 26.5 %select_add_fusion.8 = f32[3,16,132,260]{3,2,1,0:T(8,128)} fusion(f32[3,16,132,260]{3,2,1,0:T(8,128)} %get-tuple-element.2046, pred[]{:T(512)S(6)} %compare.115, f32[132,512]{1,0:T(8,128)S(1)} %select_add_fusion.6, f32[3,16,512]{2,1,0:T(8,128)S(1)} %broadcast_multiply_fusion.2, f32[512]{0:T(512)S(1)} %get-tuple-element.2026, ...), kind=kOutput, calls=%fused_computation.364.clone.1 | convolution fusion | flops 10129383424 | bytes 13563905 | tf_op jit(solution)/shard_map/while/body/eval_jaxpr/czxb,by->czxy/dot_general | solution.py:63
  528.0 26.5 %select_add_fusion.8 = f32[3,16,132,260]{3,2,1,0:T(8,128)} fusion(f32[3,16,132,260]{3,2,1,0:T(8,128)} %get-tuple-element.2046, pred[]{:T(512)S(6)} %compare.115, f32[132,512]{1,0:T(8,128)S(1)} %select_add_fusion.6, f32[3,16,512]{2,1,0:T(8,128)S(1)} %broadcast_multiply_fusion.2, f32[512]{0:T(512)S(1)} %get-tuple-element.2026, ...), kind=kOutput, calls=%fused_computation.364.clone.1 | convolution fusion | flops 10129383424 | bytes 13563905 | tf_op jit(solution)/shard_map/while/body/eval_jaxpr/czxb,by->czxy/dot_general | solution.py:63
  554.9 26.5 %select_add_fusion.8 = f32[3,16,132,260]{3,2,1,0:T(8,128)} fusion(f32[3,16,132,260]{3,2,1,0:T(8,128)} %get-tuple-element.2046, pred[]{:T(512)S(6)} %compare.115, f32[132,512]{1,0:T(8,128)S(1)} %select_add_fusion.6, f32[3,16,512]{2,1,0:T(8,128)S(1)} %broadcast_multiply_fusion.2, f32[512]{0:T(512)S(1)} %get-tuple-element.2026, ...), kind=kOutput, calls=%fused_computation.364.clone.1 | convolution fusion | flops 10129383424 | bytes 13563905 | tf_op jit(solution)/shard_map/while/body/eval_jaxpr/czxb,by->czxy/dot_general | solution.py:63
  581.8 26.5 %select_add_fusion.8 = f32[3,16,132,260]{3,2,1,0:T(8,128)} fusion(f32[3,16,132,260]{3,2,1,0:T(8,128)} %get-tuple-element.2046, pred[]{:T(512)S(6)} %compare.115, f32[132,512]{1,0:T(8,128)S(1)} %select_add_fusion.6, f32[3,16,512]{2,1,0:T(8,128)S(1)} %broadcast_multiply_fusion.2, f32[512]{0:T(512)S(1)} %get-tuple-element.2026, ...), kind=kOutput, calls=%fused_computation.364.clone.1 | convolution fusion | flops 10129383424 | bytes 13563905 | tf_op jit(solution)/shard_map/while/body/eval_jaxpr/czxb,by->czxy/dot_general | solution.py:63
  651.4 13.5 %pad_maximum_fusion = f32[3,16,136,264]{3,2,1,0:T(8,128)} fusion(f32[3,16,136,2]{3,2,1,0:T(8,128)} %copy.56, f32[3,16,2,260]{3,2,1,0:T(2,128)} %collective-permute-done.1, f32[3,16,132,260]{3,2,1,0:T(8,128)} %get-tuple-element.658, f32[3,16,2,260]{3,2,1,0:T(2,128)S(1)} %collective-permute-done, f32[3,16,136,2]{3,2,1,0:T(8,128)S(1)} %copy.55), kind=kLoop, calls=%fused_computation.465 | loop fusion | flops 6893568 | bytes 13787136 | tf_op jit(solution)/shard_map/concatenate | solution.py:17
  690.1 15.0 %scatter-add.16 = f32[3,16,128,256]{3,2,1,0:T(8,128)} dynamic-update-slice(f32[3,16,128,256]{3,2,1,0:T(8,128)} %slice.3922, f32[3,16,128,2]{3,2,1,0:T(8,128)S(1)} %slice_add_fusion.1, s32[]{:T(128)} %constant.1084.clone.1, s32[]{:T(128)} %constant.1084.clone.1, s32[]{:T(128)} %constant.1084.clone.1, s32[]{:T(128)} %constant.1084.clone.1) | dynamic-update-slice | bytes 98308 | tf_op jit(solution)/shard_map/scatter-add | solution.py:71
  709.8 10.7 %scatter-add.19 = f32[3,16,128,256]{3,2,1,0:T(8,128)} dynamic-update-slice(f32[3,16,128,256]{3,2,1,0:T(8,128)} %scatter-add.16, f32[3,16,128,1]{3,2,1,0:T(8,128)S(1)} %slice_add_fusion, s32[]{:T(128)} %constant.1084.clone.1, s32[]{:T(128)} %constant.1084.clone.1, s32[]{:T(128)} %constant.1084.clone.1, s32[]{:T(128)} %constant.1093.clone.1) | dynamic-update-slice | bytes 49156 | tf_op jit(solution)/shard_map/scatter-add | solution.py:72
  752.8 16.2 %fusion.221 = f32[3,16,128,256]{3,2,1,0:T(8,128)S(1)} fusion(f32[3,16,2,256]{3,2,1,0:T(2,128)} %copy-done.11, f32[3,16,128,256]{3,2,1,0:T(8,128)} %copy-done.4, f32[3,16,2,256]{3,2,1,0:T(2,128)S(1)} %collective-permute-done.4, f32[128,128]{1,0:T(8,128)S(1)} %copy-done.10), kind=kOutput, calls=%fused_computation.505 | convolution fusion | flops 2430074880 | bytes 12845056 | tf_op jit(solution)/shard_map/ij,czjy->cziy/dot_general | solution.py:86
  777.1 16.3 %pad_maximum_fusion.1 = (f32[3,16,132,258]{3,2,1,0:T(8,128)}, f32[3,16,132,258]{3,2,1,0:T(8,128)}) fusion(f32[3,16,132,2]{3,2,1,0:T(8,128)S(1)} %copy.58, f32[3,16,2,256]{3,2,1,0:T(2,128)S(1)} %collective-permute-done.4, f32[3,16,128,256]{3,2,1,0:T(8,128)} %copy-done.4, f32[3,16,2,256]{3,2,1,0:T(2,128)} %copy-done.11, f32[3,16,132,2]{3,2,1,0:T(8,128)} %copy.60), kind=kLoop, calls=%fused_computation.466 | loop fusion | flops 9808128 | bytes 19666944 | tf_op jit(solution)/shard_map/concatenate | solution.py:17
  793.4 16.2 %fusion.206 = f32[3,16,128,256]{3,2,1,0:T(8,128)S(1)} fusion(f32[3,16,132,258]{3,2,1,0:T(8,128)} %get-tuple-element.1167, f32[3,16,132,258]{3,2,1,0:T(8,128)} %get-tuple-element.1166, f32[256,256]{1,0:T(8,128)} %concatenate.118), kind=kOutput, calls=%fused_computation.482 | convolution fusion | flops 4839702528 | bytes 31719424 | tf_op jit(solution)/shard_map/ij,czxj->czxi/dot_general | solution.py:87
  (466 shorter events, 257.1 us)
Async XLA Ops:
  0.6 230.8 %copy-start = (f32[2048]{0:T(1024)S(1)}, f32[2048]{0:T(1024)}, u32[]{:S(2)}) copy-start(f32[2048]{0:T(1024)} %param.37) | copy-start | bytes 24580
  27.2 345.3 %all-to-all-start.1 = ((s32[1,128,32]{2,0,1:T(1,128)}), s32[1,128,32]{2,0,1:T(1,128)S(1)}, u32[]{:S(2)}, u32[]{:S(2)}) async-start(s32[1,128,32]{2,0,1:T(1,128)} %bitcast.395), calls=%async_computation.1 | async-start | bytes 131072 | tf_op jit(solution)/shard_map/all_to_all | solution.py:188
  53.8 165.6 %copy-start.13 = (f32[3,2048]{1,0:T(4,128)S(1)}, f32[3,2048]{1,0:T(4,128)}, u32[]{:S(2)}) copy-start(f32[3,2048]{1,0:T(4,128)} %param.39) | copy-start | bytes 73732
  53.8 165.6 %copy-start.14 = (f32[3,2048]{1,0:T(4,128)S(1)}, f32[3,2048]{1,0:T(4,128)}, u32[]{:S(2)}) copy-start(f32[3,2048]{1,0:T(4,128)} %param.38) | copy-start | bytes 73732
  62.6 238.9 %copy-start.12 = (f32[3,32,128]{2,1,0:T(8,128)}, f32[3,32,128]{2,1,0:T(8,128)S(1)}, u32[]{:S(2)}) copy-start(f32[3,32,128]{2,1,0:T(8,128)S(1)} %get-tuple-element.659) | copy-start | bytes 147460
  219.8 163.1 %copy-start.2 = (f32[2048]{0:T(1024)S(1)}, f32[2048]{0:T(1024)}, u32[]{:S(2)}) copy-start(f32[2048]{0:T(1024)} %param.36) | copy-start | bytes 24580
  306.4 76.4 %copy-start.16 = (f32[128]{0:T(128)}, f32[128]{0:T(128)S(1)}, u32[]{:S(2)}) copy-start(f32[128]{0:T(128)S(1)} %get-tuple-element.941) | copy-start | bytes 1540
  309.6 85.1 %copy-start.18 = (f32[128]{0:T(128)}, f32[128]{0:T(128)S(1)}, u32[]{:S(2)}) copy-start(f32[128]{0:T(128)S(1)} %get-tuple-element.943) | copy-start | bytes 1540
  312.8 72.0 %copy-start.19 = (f32[128]{0:T(128)}, f32[128]{0:T(128)S(1)}, u32[]{:S(2)}) copy-start(f32[128]{0:T(128)S(1)} %get-tuple-element.945) | copy-start | bytes 1540
  316.1 68.8 %copy-start.20 = (f32[128]{0:T(128)}, f32[128]{0:T(128)S(1)}, u32[]{:S(2)}) copy-start(f32[128]{0:T(128)S(1)} %get-tuple-element.947) | copy-start | bytes 1540
  319.4 65.5 %copy-start.21 = (f32[128]{0:T(128)}, f32[128]{0:T(128)S(1)}, u32[]{:S(2)}) copy-start(f32[128]{0:T(128)S(1)} %get-tuple-element.949) | copy-start | bytes 1540
  322.6 62.2 %copy-start.22 = (f32[128]{0:T(128)}, f32[128]{0:T(128)S(1)}, u32[]{:S(2)}) copy-start(f32[128]{0:T(128)S(1)} %get-tuple-element.951) | copy-start | bytes 1540
  325.9 68.9 %copy-start.23 = (f32[128]{0:T(128)}, f32[128]{0:T(128)S(1)}, u32[]{:S(2)}) copy-start(f32[128]{0:T(128)S(1)} %get-tuple-element.953) | copy-start | bytes 1540
  329.0 65.7 %copy-start.24 = (f32[128]{0:T(128)}, f32[128]{0:T(128)S(1)}, u32[]{:S(2)}) copy-start(f32[128]{0:T(128)S(1)} %get-tuple-element.955) | copy-start | bytes 1540
  332.1 62.6 %copy-start.25 = (f32[128]{0:T(128)}, f32[128]{0:T(128)S(1)}, u32[]{:S(2)}) copy-start(f32[128]{0:T(128)S(1)} %get-tuple-element.957) | copy-start | bytes 1540
  335.4 59.3 %copy-start.26 = (f32[128]{0:T(128)}, f32[128]{0:T(128)S(1)}, u32[]{:S(2)}) copy-start(f32[128]{0:T(128)S(1)} %get-tuple-element.959) | copy-start | bytes 1540
  338.6 56.1 %copy-start.27 = (f32[128]{0:T(128)}, f32[128]{0:T(128)S(1)}, u32[]{:S(2)}) copy-start(f32[128]{0:T(128)S(1)} %get-tuple-element.961) | copy-start | bytes 1540
  371.5 243.5 %copy-start.31 = (f32[256]{0:T(256)}, f32[256]{0:T(256)S(1)}, u32[]{:S(2)}) copy-start(f32[256]{0:T(256)S(1)} %get-tuple-element.876) | copy-start | bytes 3076
  372.5 20.3 %all-to-all-start = ((f32[128,1,192]{2,1,0:T(1,128)}), f32[128,1,192]{2,1,0:T(1,128)S(1)}, u32[]{:S(2)}, u32[]{:S(2)}) async-start(f32[128,1,192]{2,1,0:T(1,128)} %reshape.1898), calls=%async_computation | async-start | bytes 262144 | tf_op jit(solution)/shard_map/all_to_all | solution.py:187
  394.7 220.3 %copy-start.9 = (f32[7,32,256]{2,1,0:T(8,128)S(1)}, f32[7,32,256]{2,1,0:T(8,128)}, u32[]{:S(2)}) copy-start(f32[7,32,256]{2,1,0:T(8,128)} %copy-done.8) | copy-start | bytes 688132
  609.6 8.6 %collective-permute-start = (f32[3,16,2,260]{3,2,1,0:T(2,128)S(1)}, f32[3,16,2,260]{3,2,1,0:T(2,128)S(1)}, u32[]{:S(2)}, u32[]{:S(2)}) collective-permute-start(f32[3,16,2,260]{3,2,1,0:T(2,128)S(1)} %get-tuple-element.1162), channel_id=1, source_target_pairs={{0,8},{8,16},{16,24},{24,32},{32,40},{40,48},{48,56},{56,64},{64,7... | collective-permute-start | bytes 299528 | tf_op jit(solution)/shard_map/ppermute | solution.py:19
  610.1 8.1 collective-permute-start.1
  628.2 18.0 %collective-permute-start.2 = (f32[3,16,136,2]{2,1,3,0:T(8,128)}, f32[3,16,136,2]{2,1,3,0:T(8,128)}, u32[]{:S(2)}, u32[]{:S(2)}) collective-permute-start(f32[3,16,136,2]{2,1,3,0:T(8,128)} %copy.53), channel_id=1, source_target_pairs={{0,1},{1,2},{2,3},{3,4},{4,5},{5,6},{6,7},{7,0},{8,9},{9,10},{10,1... | collective-permute-start | bytes 156680 | tf_op jit(solution)/shard_map/ppermute | solution.py:19
  632.1 16.1 %collective-permute-start.3 = (f32[3,16,136,2]{2,1,3,0:T(8,128)}, f32[3,16,136,2]{2,1,3,0:T(8,128)}, u32[]{:S(2)}, u32[]{:S(2)}) collective-permute-start(f32[3,16,136,2]{2,1,3,0:T(8,128)} %copy.54), channel_id=1, source_target_pairs={{1,0},{2,1},{3,2},{4,3},{5,4},{6,5},{7,6},{0,7},{9,8},{10,9},{11,1... | collective-permute-start | bytes 156680 | tf_op jit(solution)/shard_map/ppermute | solution.py:21
  726.7 6.6 collective-permute-start.4
  731.6 6.8 collective-permute-start.5
  745.9 25.7 %collective-permute-start.8 = (f32[3,16,132,2]{2,1,3,0:T(8,128)}, f32[3,16,132,2]{2,1,3,0:T(8,128)}, u32[]{:S(2)}, u32[]{:S(2)}) collective-permute-start(f32[3,16,132,2]{2,1,3,0:T(8,128)} %copy.57), channel_id=1, source_target_pairs={{1,0},{2,1},{3,2},{4,3},{5,4},{6,5},{7,6},{0,7},{9,8},{10,9},{11,1... | collective-permute-start | bytes 152072 | tf_op jit(solution)/shard_map/ppermute | solution.py:21
  752.8 21.1 %collective-permute-start.9 = (f32[3,16,132,2]{2,1,3,0:T(8,128)}, f32[3,16,132,2]{2,1,3,0:T(8,128)}, u32[]{:S(2)}, u32[]{:S(2)}) collective-permute-start(f32[3,16,132,2]{2,1,3,0:T(8,128)} %copy.59), channel_id=1, source_target_pairs={{0,1},{1,2},{2,3},{3,4},{4,5},{5,6},{6,7},{7,0},{8,9},{9,10},{10,1... | collective-permute-start | bytes 152072 | tf_op jit(solution)/shard_map/ppermute | solution.py:19
  769.0 46.6 %collective-permute-start.6 = (f32[3,16,1,256]{3,2,1,0:T(1,128)S(1)}, f32[3,16,1,256]{3,2,1,0:T(1,128)}, u32[]{:S(2)}, u32[]{:S(2)}) collective-permute-start(f32[3,16,1,256]{3,2,1,0:T(1,128)S(1)} %slice.3998), channel_id=1, source_target_pairs={{0,8},{8,16},{16,24},{24,32},{32,40},{40,48},{48,56},{56,64},{64,7... | collective-permute-start | bytes 147464 | tf_op jit(solution)/shard_map/ppermute | solution.py:19
  815.6 5.6 collective-permute-start.10
  816.8 13.4 %collective-permute-start.7 = (f32[3,16,1,256]{3,2,1,0:T(1,128)S(1)}, f32[3,16,1,256]{3,2,1,0:T(1,128)S(1)}, u32[]{:S(2)}, u32[]{:S(2)}) collective-permute-start(f32[3,16,1,256]{3,2,1,0:T(1,128)S(1)} %get-tuple-element.1171), channel_id=1, source_target_pairs={{8,0},{16,8},{24,16},{32,24},{40,32},{48,40},{56,48},{64,56},{72,6... | collective-permute-start | bytes 147464 | tf_op jit(solution)/shard_map/ppermute | solution.py:21
  820.2 3.3 collective-permute-start.11
  (21 other events, 343.4 us)
where the time goes:
time: 852 us; the launch traced here: 839 us
  other arithmetic  350 us (41%)
  matrix products  242 us (28%)
  local copies, waits for them, and re-layouts  166 us (19%)
  starting transfers between devices  40.6 us (5%)
  waiting for transfers between devices  15.9 us (2%)
  loops' own time  15.6 us (2%)
    sub x11, other arithmetic, band_inverse(): lax.linalg.tridiagonal_solve(lower, middle, upper, jnp.eye(length, dtype=...  221 us
    dot_general x8, matrix products, spread_block(): jnp.einsum('czxb,by->czxy', scaled, table_y, precision=lax.Precision.HIGH...  210 us
    broadcast_in_dim x18, other arithmetic, band_inverse(): lax.linalg.tridiagonal_solve(lower, middle, upper, jnp.eye(length, dtype=...  49.6 us
    concatenate x3, other arithmetic, with_halo(): jnp.concatenate([lax.ppermute(tail, axis, [(i, (i + 1) % count) for i in...  30.7 us
    gather x2, local copies, waits for them, and re-layouts, local(): out_codes = jnp.where(live, jnp.take(codes, picked), 0)[None, :]  23.1 us
    slice x62, local copies, waits for them, and re-layouts, band_inverse(): lax.linalg.tridiagonal_solve(lower, middle, upper, jnp.eye(length, dtype=...  21.7 us
  transfers between devices with their start and end apart: 14, of which 4 were waited for; matrix products, arithmetic and copies ran while one was open for 49% of the time, Pallas kernels for 0%

commit v1 on v0

v1 whole, which is shorter than its diff:
```python
import functools
import math

import jax
import jax.numpy as jnp
import numpy as np
from jax import lax
from jax.experimental import pallas as pl
from jax.experimental.pallas import tpu as pltpu
from jax.sharding import PartitionSpec as P

SLOTS = 32
HALF = 0.5
GROUP = 42
BASES = 39
OFF = 8
XEXT = 144
ZEXT = 19
TILES = 7
COPIES = 2
ROOT = (math.sqrt(5.0) - 3.0) / 2.0
MESH = pl.DeviceIdType.MESH
VMEM = pltpu.VMEM
F32 = jnp.float32
BF16 = jnp.bfloat16


SCALE = 1.0 / (1.0 + 2.0 * ROOT / 3.0)
LEAD = SCALE * (7.0 / 9.0 * (1.0 / ROOT - ROOT) + 1.0 / 36.0 * (1.0 / ROOT**2 - ROOT**2))
NEAR = SCALE / 36.0 * (ROOT - 1.0 / ROOT)


def line_matrix(n):
    gap = np.arange(n)[None, :] - np.arange(n)[:, None]
    out = np.sign(gap) * LEAD * ROOT ** np.abs(gap).astype(np.float64)
    return out + np.where(np.abs(gap) == 1, np.sign(gap) * NEAR, 0.0)


def halo_columns(n):
    out = np.zeros((n, 4))
    steps = np.arange(n)
    out[:, 0] = -LEAD * ROOT ** (steps + 1.0)
    out[0, 1] = -NEAR
    out[:, 2] = LEAD * ROOT ** (n - steps * 1.0)
    out[n - 1, 3] = NEAR
    return out


def halves(values):
    values = np.asarray(values, np.float32)
    high = values.astype(BF16)
    low = (values - high.astype(np.float32)).astype(BF16)
    return high, low


def split(x):
    high = x.astype(BF16)
    return high, (x - high.astype(F32)).astype(BF16)


def dot(a, b):
    return jnp.dot(a, b, preferred_element_type=F32)


def edge_weights(n, total):
    out = np.zeros((8, total))
    steps = np.arange(n)
    out[0, :n] = ROOT ** (n - 1.0 - steps)
    out[1, n - 1] = 1.0
    out[2, n] = 1.0
    out[3, n + 1] = 1.0
    out[4, :n] = ROOT ** (steps * 1.0)
    out[5, 0] = 1.0
    out[6, n + 2] = 1.0
    return out


def pack_kernel(counts_ref, table_ref, out_ref, wide):
    size = table_ref.shape[1]
    wide[:, 0:size] = table_ref[...]
    wide[:, size:] = jnp.zeros((8, wide.shape[1] - size), F32)
    lane = lax.broadcasted_iota(jnp.int32, (8, 128), 1)
    sub = lax.broadcasted_iota(jnp.int32, (8, 128), 0)
    part = sub & 3

    def one(d, start):
        count = counts_ref[0, d]
        first = pl.multiple_of((start >> 7) << 7, 128)
        shift = start & 127
        back = (128 - shift) & 127
        a = pltpu.roll(wide[:, pl.ds(first, 128)], back, 1)
        b = pltpu.roll(wide[:, pl.ds(first + 128, 128)], back, 1)
        w = jnp.where(lane + shift < 128, a, b)
        w = jnp.where(lane < count, w, 0.0)
        m = w
        for j in range(1, 4):
            m = jnp.where(part == j, pltpu.roll(w, SLOTS * j, 1), m)
        top = jnp.sum(jnp.where(sub < 4, m, 0.0), axis=0, keepdims=True)
        low = jnp.sum(jnp.where(sub < 4, 0.0, m), axis=0, keepdims=True)
        return start + count, top, low

    def eight(g, start):
        tops, lows = [], []
        for k in range(8):
            start, top, low = one(g * 8 + k, start)
            tops.append(top)
            lows.append(low)
        at = pl.multiple_of(g * 8, 8)
        out_ref[pl.ds(at, 8), 0:128] = jnp.concatenate(tops, axis=0)
        out_ref[pl.ds(at, 8), 128:256] = jnp.concatenate(lows, axis=0)
        return start

    lax.fori_loop(0, out_ref.shape[0] // 8, eight, jnp.int32(0))


def pack(counts, table):
    blocks = counts.shape[1]
    return pl.pallas_call(
        pack_kernel,
        out_shape=jax.ShapeDtypeStruct((blocks, 256), F32),
        in_specs=[pl.BlockSpec(memory_space=pltpu.SMEM), pl.BlockSpec(memory_space=VMEM)],
        out_specs=pl.BlockSpec(memory_space=VMEM),
        scratch_shapes=[VMEM((8, table.shape[1] + 256), F32)],
        name="pack",
    )(counts, table)


def spread_kernel(
    inbox_ref, mx_ref, my_ref, sel0_ref, sel1_ref, selr_ref, pick_ref, tail_ref, wfar_ref, wnear_ref, v_hbm,
    e_hbm, rl_ref, cn_ref, ud_ref,
    *scratch,
):
    grids = scratch[:COPIES]
    vbuf, m8, wz_v, base_v, wz_s, base_s, fcy, mxcol, rlp, udp, v_sem, e_sems, s_sems = scratch[COPIES:]
    sources = inbox_ref.shape[0]
    total = sources * SLOTS
    chunks = total // 128
    vin = pltpu.make_async_copy(v_hbm, vbuf, v_sem)
    vin.start()
    lane = lax.broadcasted_iota(jnp.int32, (8, 128), 1)
    sub = lax.broadcasted_iota(jnp.int32, (8, 128), 0)

    def regroup(pair, carry):
        rows = inbox_ref[pl.ds(pl.multiple_of(pair * 8, 8), 8), :]
        four(pair * 2, rows[0:4])
        four(pair * 2 + 1, rows[4:8])
        return carry

    def four(g, rows):
        out = None
        for k in range(4):
            row = rows[k : k + 1]
            x = jnp.where(
                sub < 4, jnp.broadcast_to(row[:, 0:128], (8, 128)), jnp.broadcast_to(row[:, 128:256], (8, 128))
            )
            y = x
            for j in range(4):
                turn = (SLOTS * (k - j)) % 128
                z = pltpu.roll(x, turn, 1) if turn else x
                y = jnp.where((sub & 3) == j, z, y)
            out = y if out is None else jnp.where((lane >> 5) == k, y, out)
        at = pl.multiple_of(g * 128, 128)
        m8[:, pl.ds(at, 128)] = out
        root = jnp.sqrt(jnp.maximum(1.0 + 4.0 * out - 4.0 * out * out, 0.0))
        frac = out
        ws = (
            (3.0 - 2.0 * frac - root) / 8.0,
            (3.0 - 2.0 * frac + root) / 8.0,
            (1.0 + 2.0 * frac + root) / 8.0,
            (1.0 + 2.0 * frac - root) / 8.0,
        )
        wz_v[:, pl.ds(at, 128)] = jnp.concatenate([w[5:6] for w in ws] + [jnp.zeros((4, 128), F32)], axis=0)
        code = out[6:7].astype(jnp.int32)
        cell_z = code & 15
        cell_y = (code >> 4) & 255
        cell_x = code >> 12
        tile = (cell_y * 1681) >> 16
        base = (tile * ZEXT + cell_z) * XEXT + cell_x + (OFF - 1)
        base_v[:, pl.ds(at, 128)] = jnp.broadcast_to(base, (8, 128))

    lax.fori_loop(0, chunks // 2, regroup, 0)
    c1 = pltpu.make_async_copy(wz_v, wz_s, s_sems.at[0])
    c2 = pltpu.make_async_copy(base_v, base_s, s_sems.at[1])
    c1.start()
    c2.start()

    rows = grids[0].shape[0]
    step = 152

    def clear(i, carry):
        for grid in grids:
            grid[pl.ds(pl.multiple_of(i * step, 8), step), :] = jnp.zeros((step, 128), F32)
        return carry

    lax.fori_loop(0, rows // step, clear, 0)
    c1.wait()
    c2.wait()

    lane2 = lax.broadcasted_iota(jnp.int32, (128, 128), 1)
    comp = jnp.where(lane2 >= 2 * GROUP, 2, jnp.where(lane2 >= GROUP, 1, 0))
    rel = jnp.where(lane2 >= 3 * GROUP, -100, lane2 - GROUP * comp).astype(F32)

    def chunk(c, carry):
        at = pl.multiple_of(c * 128, 128)
        m = m8[:, pl.ds(at, 128)]
        root = jnp.sqrt(jnp.maximum(1.0 + 4.0 * m - 4.0 * m * m, 0.0))
        ws = (
            (3.0 - 2.0 * m - root) / 8.0,
            (3.0 - 2.0 * m + root) / 8.0,
            (1.0 + 2.0 * m + root) / 8.0,
            (1.0 + 2.0 * m - root) / 8.0,
        )
        code = m[6:7].astype(jnp.int32)
        cell_y = (code >> 4) & 255
        tile = (cell_y * 1681) >> 16
        inner = (cell_y - BASES * tile).astype(F32)
        block = jnp.concatenate([m[0:3], inner] + [w[4:5] for w in ws] + [jnp.zeros((120, 128), F32)], axis=0)
        cols = jnp.transpose(block)
        col = lambda i: jnp.broadcast_to(cols[:, i : i + 1], (128, 128))
        d = rel - col(3)
        w = jnp.where(d == 0.0, col(4), 0.0)
        w = jnp.where(d == 1.0, col(5), w)
        w = jnp.where(d == 2.0, col(6), w)
        w = jnp.where(d == 3.0, col(7), w)
        f = jnp.where(comp == 0, col(0), jnp.where(comp == 1, col(1), col(2)))
        fcy[...] = w * f
        wx = jnp.concatenate([w[3:4] for w in ws] + [jnp.zeros((4, 128), F32)], axis=0)

        def eight(g, wx):
            for k0 in range(0, 8, COPIES):
                loads = []
                for k in range(k0, k0 + COPIES):
                    idx = c * 128 + g * 8 + k
                    b = base_s[0, idx]
                    p = wx[:, k : k + 1] * fcy[pl.ds(g * 8 + k, 1), :]
                    grid = grids[k % COPIES]
                    loads.append(
                        [
                            (grid, b + dz * XEXT, grid[pl.ds(b + dz * XEXT, 8), :] + wz_s[dz, idx] * p)
                            for dz in range(4)
                        ]
                    )
                for group in loads:
                    for grid, at, value in group:
                        grid[pl.ds(at, 8), :] = value
            return pltpu.roll(wx, 120, 1)

        lax.fori_loop(0, 16, eight, wx)
        return carry

    lax.fori_loop(0, chunks, chunk, 0)

    for t in range(TILES):
        for src, dst in ((0, 16), (17, 1), (18, 2)):
            i, j = (t * ZEXT + src) * XEXT, (t * ZEXT + dst) * XEXT
            moved = grids[0][i : i + XEXT, :]
            for grid in grids[1:]:
                moved = moved + grid[i : i + XEXT, :]
            grids[0][j : j + XEXT, :] += moved

    mrow = mx_ref[0:1, :]
    mxcol[0:128, :] = jnp.transpose(jnp.broadcast_to(mrow[:, 0:128], (128, 128)))
    mxcol[128:144, :] = jnp.transpose(jnp.broadcast_to(mrow[:, 128:256], (128, 128)))[0:16]
    vin.wait()

    def plane(z, carry):
        highs, lows = [], []
        for t in range(TILES):
            at = pl.multiple_of((t * ZEXT + z + 1) * XEXT, 8)
            x = grids[0][pl.ds(at, XEXT), :]
            for grid in grids[1:]:
                x = x + grid[pl.ds(at, XEXT), :]
            high, low = split(x)
            highs.append(high)
            lows.append(low)
        outs = []
        for tiles, sel in (((0, 1, 2, 3), sel0_ref), ((3, 4, 5, 6), sel1_ref), ((0, 6), selr_ref)):
            high = jnp.concatenate([highs[t] for t in tiles], axis=1)
            low = jnp.concatenate([lows[t] for t in tiles], axis=1)
            outs.append(dot(high, sel[...]) + dot(low, sel[...]))
        mcol = mxcol[...]
        far, near = wfar_ref[...], wnear_ref[...]
        for c in range(3):
            p = c * 16 + z
            ext = []
            for h in range(3):
                e = outs[h][:, c * 128 : (c + 1) * 128] * mcol * my_ref[0:1, h * 128 : (h + 1) * 128]
                if h < 2:
                    inner = e[OFF : OFF + 128] + vbuf[c, z, :, h * 128 : (h + 1) * 128]
                    vbuf[c, z, :, h * 128 : (h + 1) * 128] = inner
                    e = jnp.concatenate([e[0:OFF], inner, e[OFF + 128 :]], axis=0)
                ext.append(e)
                rowset = [
                    jnp.sum(e * far, axis=0, keepdims=True),
                    e[OFF + 127 : OFF + 130],
                    jnp.sum(e * near, axis=0, keepdims=True),
                    e[OFF : OFF + 1],
                    e[OFF - 1 : OFF],
                    jnp.zeros((1, 128), F32),
                ]
                rlp[h, pl.ds(pl.multiple_of(p * 8, 8), 8), :] = jnp.concatenate(rowset, axis=0)
            high, low = split(jnp.concatenate([e[OFF : OFF + 128] for e in ext], axis=1))
            nt = (((1,), (1,)), ((), ()))
            one = lax.dot_general(pick_ref[...], high, nt, preferred_element_type=F32)
            two = lax.dot_general(pick_ref[...], low, nt, preferred_element_type=F32)
            udp[pl.ds(pl.multiple_of(p * 8, 8), 8), :] = one[0:8] + one[8:16] + two[0:8]
        pltpu.make_async_copy(vbuf.at[:, z], e_hbm.at[:, z], e_sems.at[z]).start()
        return carry

    lax.fori_loop(0, 16, plane, 0)

    corner = jnp.zeros((48, 128), F32)
    for t in range(7):
        row = jnp.concatenate([rlp[h, pl.ds(t, 48, stride=8), :] for h in range(3)], axis=1)
        rl_ref[t] = row[:, 0:256]
        ends = jnp.dot(row, tail_ref[...], preferred_element_type=F32, precision=lax.Precision.HIGHEST)
        corner = corner + (pltpu.roll(ends, 8 * t, 1) if t else ends)
        ud_ref[t] = udp[pl.ds(t, 48, stride=8), :]
    rl_ref[7] = jnp.zeros((48, 256), F32)
    ud_ref[7] = jnp.zeros((48, 128), F32)
    cn_ref[...] = corner
    for z in range(16):
        pltpu.make_async_copy(vbuf.at[:, z], e_hbm.at[:, z], e_sems.at[z]).wait()


def selectors():
    pick = {}
    for name, tiles, first in (("a", (0, 1, 2, 3), 0), ("b", (3, 4, 5, 6), 128)):
        out = np.zeros((4 * 128, 3 * 128), np.float32)
        for i, t in enumerate(tiles):
            for c in range(3):
                for j in range(GROUP):
                    y = BASES * t - 1 + j - first
                    if 0 <= y < 128:
                        out[i * 128 + c * GROUP + j, c * 128 + y] = 1.0
        pick[name] = out.astype(BF16)
    out = np.zeros((2 * 128, 3 * 128), np.float32)
    for i, t in enumerate((0, 6)):
        for c in range(3):
            for j in range(GROUP):
                y = BASES * t - 1 + j
                spot = {256: 0, 257: 1, -1: 2}.get(y)
                if spot is not None:
                    out[i * 128 + c * GROUP + j, c * 128 + spot] = 1.0
    return pick["a"], pick["b"], out.astype(BF16)


def spread(inbox, mx, my, v):
    sel0, sel1, selr = selectors()
    ends = edge_weights(256, 384)
    high, low = halves(ends)
    pick = np.concatenate([high, low], axis=0)
    tail = np.zeros((384, 128), np.float32)
    tail[:, 0:8] = ends.T
    weights = edge_weights(128, 144)
    far = np.zeros((XEXT, 128), np.float32)
    near = np.zeros((XEXT, 128), np.float32)
    far[OFF : OFF + 128] = weights[0, 0:128, None]
    near[OFF : OFF + 128] = weights[4, 0:128, None]
    rows = TILES * ZEXT * XEXT
    total = inbox.shape[0] * SLOTS
    vm = pl.BlockSpec(memory_space=VMEM)
    return pl.pallas_call(
        spread_kernel,
        out_shape=(
            jax.ShapeDtypeStruct(v.shape, F32),
            jax.ShapeDtypeStruct((8, 48, 256), F32),
            jax.ShapeDtypeStruct((48, 128), F32),
            jax.ShapeDtypeStruct((8, 48, 128), F32),
        ),
        in_specs=[vm] * 10 + [pl.BlockSpec(memory_space=pl.ANY)],
        out_specs=(pl.BlockSpec(memory_space=pl.ANY), vm, vm, vm),
        scratch_shapes=[VMEM((rows, 128), F32)] * COPIES
        + [
            VMEM(v.shape, F32),
            VMEM((8, total), F32),
            VMEM((8, total), F32),
            VMEM((8, total), jnp.int32),
            pltpu.SMEM((8, total), F32),
            pltpu.SMEM((8, total), jnp.int32),
            VMEM((128, 128), F32),
            VMEM((XEXT, 128), F32),
            VMEM((3, 48 * 8, 128), F32),
            VMEM((48 * 8, 128), F32),
            pltpu.SemaphoreType.DMA,
            pltpu.SemaphoreType.DMA((16,)),
            pltpu.SemaphoreType.DMA((2,)),
        ],
        compiler_params=pltpu.CompilerParams(vmem_limit_bytes=56 << 20),
        name="spread",
    )(inbox, mx, my, sel0, sel1, selr, pick, tail, far, near, v)


def exchange_kernel(
    rl_ref, cn_ref, ud_ref, xh_ref, yh_ref, ra, ca, rb, cb, umsg, hmsg, pu, ph, qd, qh, send_sems, recv_sems
):
    gx, gy = lax.axis_index("gx"), lax.axis_index("gy")
    nx, ny = lax.axis_size("gx"), lax.axis_size("gy")
    right = (lax.rem(gx + 1, nx), gy)
    left = (lax.rem(gx + nx - 1, nx), gy)
    up = (gx, lax.rem(gy + 1, ny))
    down = (gx, lax.rem(gy + ny - 1, ny))
    barrier = pltpu.get_barrier_semaphore()
    for device in (right, left, up, down):
        pl.semaphore_signal(barrier, inc=1, device_id=device, device_id_type=MESH)
    pl.semaphore_wait(barrier, 4)

    def send(i, src, dst, device):
        copy = pltpu.make_async_remote_copy(
            src_ref=src, dst_ref=dst, send_sem=send_sems.at[i], recv_sem=recv_sems.at[i],
            device_id=device, device_id_type=MESH,
        )
        copy.start()
        return copy

    first = [
        send(0, cn_ref, ca, right),
        send(1, cn_ref, cb, left),
        send(2, rl_ref.at[0:4], ra, right),
        send(3, rl_ref.at[4:7], rb, left),
    ]
    planes = cn_ref.shape[0]
    lane = lax.broadcasted_iota(jnp.int32, (planes, 128), 1)
    first[0].wait()
    first[1].wait()
    own, a, b = cn_ref[...], ca[...], cb[...]
    turn = lambda x, by: pltpu.roll(x, by % 128, 1)
    hold = jnp.where(lane < 8, a + turn(own, -48), a + turn(own, -40))
    hold = jnp.where(
        lane < 16, hold, turn(b, -16) + jnp.where(lane < 24, own + ROOT * turn(own, -8), turn(own, 8))
    )
    hmsg[...] = jnp.where(lane < 32, hold, 0.0)
    for s in range(7):
        umsg[s] = (
            ud_ref[s]
            + jnp.where(lane == 0, a[:, 16 + s : 17 + s], 0.0)
            + jnp.where(lane == 1, a[:, 24 + s : 25 + s], 0.0)
            + jnp.where(lane == 127, b[:, 48 + s : 49 + s], 0.0)
        )
    second = [
        send(4, hmsg, ph, up),
        send(5, hmsg, qh, down),
        send(6, umsg.at[0:4], pu, up),
        send(7, umsg.at[4:7], qd, down),
    ]
    first[2].wait()
    first[3].wait()
    second[0].wait()
    second[1].wait()
    lane = lax.broadcasted_iota(jnp.int32, (planes, 256), 1)
    p, q = ph[...], qh[...]

    def rims(h):
        return (
            jnp.where(lane == 0, p[:, 8 * h + 2 : 8 * h + 3], 0.0)
            + jnp.where(lane == 1, p[:, 8 * h + 3 : 8 * h + 4], 0.0)
            + jnp.where(lane == 255, q[:, 8 * h + 6 : 8 * h + 7], 0.0)
        )

    def put(t, value):
        for h in range(2):
            xh_ref[h, pl.ds(t, planes, stride=8), :] = value[:, h * 128 : (h + 1) * 128]

    put(0, ra[0] + rl_ref[6] + rims(0))
    put(1, ra[1] + rl_ref[6] + rims(1))
    put(2, rb[0] + rl_ref[2] + ROOT * rl_ref[3] + rims(2))
    put(3, rb[1] + rl_ref[2] + rims(3))
    put(4, ra[2])
    put(5, ra[3])
    put(6, rb[2])
    put(7, jnp.zeros((planes, 256), F32))
    second[2].wait()
    second[3].wait()
    yh_ref[pl.ds(0, planes, stride=8), :] = pu[0] + umsg[6]
    yh_ref[pl.ds(1, planes, stride=8), :] = pu[1] + umsg[6]
    yh_ref[pl.ds(2, planes, stride=8), :] = qd[0] + umsg[2] + ROOT * umsg[3]
    yh_ref[pl.ds(3, planes, stride=8), :] = qd[1] + umsg[2]
    yh_ref[pl.ds(4, planes, stride=8), :] = pu[2]
    yh_ref[pl.ds(5, planes, stride=8), :] = pu[3]
    yh_ref[pl.ds(6, planes, stride=8), :] = qd[2]
    yh_ref[pl.ds(7, planes, stride=8), :] = jnp.zeros((planes, 128), F32)


def exchange(rl, cn, ud):
    n = cn.shape[0]
    vm = pl.BlockSpec(memory_space=VMEM)
    return pl.pallas_call(
        exchange_kernel,
        out_shape=(jax.ShapeDtypeStruct((2, 8 * n, 128), F32), jax.ShapeDtypeStruct((8 * n, 128), F32)),
        in_specs=[vm, vm, vm],
        out_specs=(vm, vm),
        scratch_shapes=[
            VMEM((4, n, 256), F32),
            VMEM((n, 128), F32),
            VMEM((3, n, 256), F32),
            VMEM((n, 128), F32),
            VMEM((7, n, 128), F32),
            VMEM((n, 128), F32),
            VMEM((4, n, 128), F32),
            VMEM((n, 128), F32),
            VMEM((3, n, 128), F32),
            VMEM((n, 128), F32),
            pltpu.SemaphoreType.DMA((8,)),
            pltpu.SemaphoreType.DMA((8,)),
        ],
        compiler_params=pltpu.CompilerParams(collective_id=0, has_side_effects=True),
        name="exchange",
    )(rl, cn, ud)


def derive_kernel(e_ref, xh_ref, yh_ref, mx_ref, my_ref, kx_ref, ky_ref, kl_ref, rim_ref, dx_ref, dy_ref, mxcol):
    step = pl.program_id(0)

    @pl.when(step == 0)
    def _():
        mxcol[...] = jnp.transpose(jnp.broadcast_to(mx_ref[0:1, :], (128, 128)))

    each = e_ref.shape[0]
    for i in range(each):
        xall = jnp.concatenate([xh_ref[0, i * 8 : i * 8 + 8, :], xh_ref[1, i * 8 : i * 8 + 8, :]], axis=1)
        yrow = yh_ref[i * 8 : i * 8 + 8, :]
        high = yrow.astype(BF16).astype(F32)
        lows = yrow - high
        stack = jnp.concatenate([high, lows, high, jnp.zeros((8, 128), F32)], axis=0).astype(BF16)
        extra = lax.dot_general(stack, rim_ref[...], (((0,), (0,)), ((), ())), preferred_element_type=F32)
        zero = jnp.zeros((1, 256), F32)
        top = jnp.concatenate([xall[4:6]] + [zero] * 6, axis=0)
        low = jnp.concatenate([zero] * 7 + [xall[6:7]], axis=0)
        e = e_ref[i]
        f = jnp.concatenate([e[0:8] + top, e[8:120], e[120:128] + low], axis=0) + extra[:, 256:512]
        halo = jnp.concatenate([xall[0:4]] + [zero] * 12, axis=0)
        fh, fl = split(f)
        hh, hl = split(halo)
        xh = jnp.concatenate([fh, hh], axis=0)
        xl = jnp.concatenate([fl, hl], axis=0)
        one = dot(kx_ref[...], xh)
        dx = one[0:128] + one[128:256] + dot(kx_ref[0:128], xl)
        col = mxcol[...]
        dx_ref[i, :, 0:128] = dx[:, 0:128] * col
        dx_ref[i, :, 128:256] = dx[:, 128:256] * col
        two = dot(jnp.concatenate([fh, fl], axis=0), ky_ref[...])
        dy = two[0:128] + two[128:256] + dot(fh, kl_ref[...]) + extra[:, 0:256]
        dy_ref[i] = dy * my_ref[0:1, :]


def derive(e, xh, yh, mx, my):
    n, rows, cols = e.shape
    each = 4
    kx = np.zeros((rows, 144))
    kx[:, 0:rows] = line_matrix(rows)
    kx[:, rows : rows + 4] = halo_columns(rows)
    kx = np.concatenate(halves(kx), axis=0)
    kh, kl = halves(line_matrix(cols).T)
    rim = np.zeros((8, 512))
    rim[0:4, 0:256] = halo_columns(cols).T
    rim[4, 256] = 1.0
    rim[5, 257] = 1.0
    rim[6, 511] = 1.0
    rh, rlow = halves(rim)
    rim = np.concatenate([rh, rh, rlow, np.zeros((8, 512), BF16)], axis=0)
    whole = lambda x: pl.BlockSpec(x.shape, lambda i: (0,) * x.ndim)
    block = pl.BlockSpec((each, rows, cols), lambda i: (i, 0, 0))
    consts = (kx, kh, kl, rim)
    return pl.pallas_call(
        derive_kernel,
        grid=(n // each,),
        out_shape=(jax.ShapeDtypeStruct(e.shape, F32),) * 2,
        in_specs=[block, pl.BlockSpec((2, each * 8, 128), lambda i: (0, i, 0)), pl.BlockSpec((each * 8, 128), lambda i: (i, 0))]
        + [whole(x) for x in (mx, my) + consts],
        out_specs=(block, block),
        scratch_shapes=[VMEM((128, 128), F32)],
        compiler_params=pltpu.CompilerParams(vmem_limit_bytes=48 << 20),
        name="derive",
    )(e, xh, yh, mx, my, *consts)


def metrics(metric_x, metric_y, gx, gy, rows, cols):
    nx, ny = metric_x.shape[0], metric_y.shape[0]
    long = jnp.concatenate([metric_x[nx - OFF :], metric_x, metric_x[: 256 - OFF]])
    mx = lax.dynamic_slice(long, (gx * rows,), (256,))
    here = lax.dynamic_slice(metric_x, (gx * rows,), (rows,))
    inner = lax.dynamic_slice(metric_y, (gy * cols,), (cols,))
    long = jnp.concatenate([metric_y[ny - 1 :], metric_y, metric_y[:2]])
    before = lax.dynamic_slice(long, (gy * cols,), (1,))
    after = lax.dynamic_slice(long, (gy * cols + cols + 1,), (2,))
    my = HALF * jnp.concatenate([inner, after, before, jnp.zeros((125,), F32)])
    wide = lambda x: jnp.broadcast_to(x[None, :], (8, x.shape[0]))
    return wide(mx), wide(my), wide(here), wide(inner)


def local(
    velocity, metric_x, metric_y, marker_force, marker_frac, marker_cell_x, marker_cell_y, marker_cell_z, send_counts
):
    comps, planes, rows, cols = velocity.shape
    gx, gy = lax.axis_index("gx"), lax.axis_index("gy")
    code = (marker_cell_x * cols + marker_cell_y) * planes + marker_cell_z
    code = code.astype(F32)[None, :]
    table = jnp.concatenate([marker_force, marker_frac, code, jnp.zeros_like(code)], axis=0)
    outbox = pack(send_counts, table)
    inbox = lax.all_to_all(outbox, ("gx", "gy"), split_axis=0, concat_axis=0, tiled=True)
    mx, my, here, inner = metrics(metric_x, metric_y, gx, gy, rows, cols)
    e, rl, cn, ud = spread(inbox, mx, my, velocity)
    xh, yh = exchange(rl, cn, ud)
    dx, dy = derive(e.reshape(comps * planes, rows, cols), xh, yh, here, inner)
    return dx.reshape(velocity.shape), dy.reshape(velocity.shape)


def solution(mesh):
    both = ("gx", "gy")
    placed = (
        P(None, None, "gx", "gy"), P(), P(), P(None, both), P(None, both), P(both), P(both), P(both), P(both, None),
    )
    return jax.shard_map(
        local,
        mesh=mesh,
        in_specs=placed,
        out_specs=(P(None, None, "gx", "gy"), P(None, None, "gx", "gy")),
        check_vma=False,
    )
```

time: 852 us -> 148 us (0.17); the launches traced: 839 us -> 147 us
  other arithmetic: 350 us -> 3.01 us
  matrix products: 242 us -> 0 us
  local copies, waits for them, and re-layouts: 166 us -> 13.4 us
  Pallas kernels: 0 us -> 117 us
  starting transfers between devices: 40.6 us -> 11.5 us
  loops' own time: 15.6 us -> 0 us
  waiting for transfers between devices: 15.9 us -> 1.44 us
    dot_general x10 -> x0, matrix products: 242 us -> none  [the longest x8 210 us: spread_block(): jnp.einsum('czxb,by->czxy', scaled, table_y, precision=lax.Precision.HIGH...]
    sub x12 -> x0, other arithmetic: 221 us -> none  [the longest x11 221 us: band_inverse(): lax.linalg.tridiagonal_solve(lower, middle, upper, jnp.eye(length, dtype=...]
    pallas_call x0 -> x4, Pallas kernels: none -> 117 us  [the longest x1 83 us: spread(): pl.pallas_call(spread_kernel, out_shape=(jax.ShapeDtypeStruct(v.shape, F3...]
    slice x94 -> x4, local copies, waits for them, and re-layouts: 64.9 us -> 3.4 us  [the longest x2 1.96 us: metrics(): long = jnp.concatenate([metric_y[ny - 1:], metric_y, metric_y[:2]])]
    broadcast_in_dim x18 -> x0, other arithmetic: 49.6 us -> none  [band_inverse(): lax.linalg.tridiagonal_solve(lower, middle, upper, jnp.eye(length, dtype=...]
    gather x6 -> x0, local copies, waits for them, and re-layouts: 38.4 us -> none  [the longest x2 23.1 us: local(): out_codes = jnp.where(live, jnp.take(codes, picked), 0)[None, :]]
    concatenate x4 -> x1, other arithmetic: 30.7 us -> 1.48 us  [local(): jnp.concatenate([marker_force, marker_frac, code, jnp.zeros_like(code)],...]
    scatter-add x3 -> x0, local copies, waits for them, and re-layouts: 28.1 us -> none  [the longest x1 15 us: fold_rims(): folded = folded.at[:, :, :, 0:2].add(inner[:, :, :, 0:2])]
  transfers between devices with their start and end apart: 14 -> 1, of which waited for: 4 -> 1; matrix products, arithmetic and copies ran while one was open for 49% -> 6% of each run, Pallas kernels for 0% -> 0%
where the time goes in v1:
time: 148 us; the launch traced here: 147 us
  Pallas kernels  117 us (79%)
  local copies, waits for them, and re-layouts  13.4 us (9%)
  starting transfers between devices  11.5 us (8%)
  other arithmetic  3.01 us (2%)
    pallas_call x1, Pallas kernels, spread(): pl.pallas_call(spread_kernel, out_shape=(jax.ShapeDtypeStruct(v.shape, F3...  83 us
    pallas_call x1, Pallas kernels, derive(): pl.pallas_call(derive_kernel, grid=(n // each,), out_shape=(jax.ShapeDtyp...  15.9 us
    pallas_call x1, Pallas kernels, exchange(): pl.pallas_call(exchange_kernel, out_shape=(jax.ShapeDtypeStruct((2, 8 * n...  13.4 us
    all_to_all x1, starting transfers between devices, local(): lax.all_to_all(outbox, ('gx', 'gy'), split_axis=0, concat_axis=0, tiled=T...  11.5 us
    pallas_call x1, Pallas kernels, pack(): pl.pallas_call(pack_kernel, out_shape=jax.ShapeDtypeStruct((blocks, 256),...  4.33 us
  transfers between devices with their start and end apart: 1, of which 1 were waited for; matrix products, arithmetic and copies ran while one was open for 6% of the time, Pallas kernels for 0%

profile of v1, /device:TPU:1, one launch (start us, length us, event | category | flops | bytes accessed | tf_op | source)
XLA Modules:
  0.0 146.8 jit_solution(4421427898357143289)
XLA Ops:
  0.6 0.0 copy-start.5
  0.6 0.0 copy-start.2
  0.7 0.0 copy-start.3
  0.7 0.0 copy-start.4
  0.7 0.1 pad.7.clone
  0.8 0.8 add_convert_fusion
  1.6 1.5 %maximum_maximum_fusion.table_ref = f32[8,2048]{1,0:T(8,128)} fusion(f32[1,2048]{1,0:T(1,128)S(1)} %bitcast.12, f32[3,2048]{1,0:T(4,128)} %param.24, f32[3,2048]{1,0:T(4,128)} %param.23, f32[8]{0:T(128)S(1)} %pad.7.clone), kind=kLoop, calls=%fused_computation.1 | loop fusion | flops 49152 | bytes 122912 | tf_op jit(solution)/shard_map/concatenate | solution.py:598
  3.0 4.3 %pack.1 = f32[128,256]{1,0:T(8,128)} custom-call(s32[1,128]{1,0:T(1,128)} %counts_ref.1, f32[8,2048]{1,0:T(8,128)} %maximum_maximum_fusion.table_ref), custom_call_target="tpu_custom_call" | custom-call | tf_op jit(solution)/shard_map/pack/pallas_call | solution.py:118
  7.4 1.7 %copy.22 = f32[128,1,256]{2,1,0:T(1,128)} copy(f32[128,1,256]{2,0,1:T(8,128)} %bitcast.11) | data formatting | bytes 262144 | tf_op jit(solution)/shard_map/all_to_all | solution.py:600
  9.1 11.5 %all-to-all-start = ((f32[128,1,256]{2,1,0:T(1,128)}), f32[128,1,256]{2,1,0:T(1,128)S(1)}, u32[]{:S(2)}, u32[]{:S(2)}) async-start(f32[128,1,256]{2,1,0:T(1,128)} %copy.22), calls=%async_computation | async-start | bytes 262144 | tf_op jit(solution)/shard_map/all_to_all | solution.py:600
  20.6 1.3 slice.14
  21.9 0.7 slice.15
  22.5 0.8 slice.12
  23.3 0.7 slice.13
  24.0 0.8 dynamic_slice.19
  24.7 0.8 dynamic_slice.16
  25.5 1.4 concatenate.18
  26.9 0.6 dynamic_slice.18
  27.5 0.1 dynamic_slice.17
  27.6 0.8 concatenate.17
  28.4 0.1 dynamic_slice.15
  28.4 0.7 maximum_multiply_fusion
  29.2 1.4 all-to-all-done
  30.6 0.7 copy.25
  31.3 0.6 broadcast_in_dim.16.mx_ref
  31.9 0.6 broadcast_in_dim.18.my_ref
  32.5 83.0 %spread.1 = (f32[3,16,128,256]{3,2,1,0:T(8,128)}, f32[8,48,256]{2,1,0:T(8,128)}, f32[48,128]{1,0:T(8,128)}, f32[8,48,128]{2,1,0:T(8,128)}) custom-call(f32[128,256]{1,0:T(8,128)} %bitcast.10, f32[8,256]{1,0:T(8,128)} %broadcast_in_dim.16.mx_ref, f32[8,384]{1,0:T(8,128)} %broadcast_in_dim.18.my_ref, bf16[512,384]{1,0:T(8,128)(2,1)} %constant.56.clone.sel0_ref, ...), custom_call_target="tpu_custom_call" | custom-call | tf_op jit(solution)/shard_map/spread/pallas_call | solution.py:363
  115.5 13.4 %exchange.1 = (f32[2,384,128]{2,1,0:T(8,128)}, f32[384,128]{1,0:T(8,128)}) custom-call(f32[8,48,256]{2,1,0:T(8,128)} %get-tuple-element.11.rl_ref, f32[48,128]{1,0:T(8,128)} %get-tuple-element.12.cn_ref, f32[8,48,128]{2,1,0:T(8,128)} %get-tuple-element.13.ud_ref), custom_call_target="tpu_custom_call" | custom-call | tf_op jit(solution)/shard_map/exchange/pallas_call | solution.py:487
  128.9 0.0 copy-done.5
  129.0 1.0 copy-done
  130.0 0.9 copy-done.1
  130.9 15.9 %derive.1 = (f32[48,128,256]{2,1,0:T(8,128)}, f32[48,128,256]{2,1,0:T(8,128)}) custom-call(f32[48,128,256]{2,1,0:T(8,128)} %bitcast.9, f32[2,384,128]{2,1,0:T(8,128)S(1)} %copy-done, f32[384,128]{1,0:T(8,128)S(1)} %copy-done.1, f32[8,128]{1,0:T(8,128)S(1)} %broadcast_in_dim.38.mx_ref, f32[8,256]{1,0:T(8,128)S(1)} %broadcast_in_dim.39.my_ref, ...), custom_call_target="tpu_custom_call" | custom-call | tf_op jit(solution)/shard_map/derive/pallas_call | solution.py:564
  (8 shorter events, 0.0 us)
Async XLA Ops:
  0.6 128.3 %copy-start.5 = (bf16[32,512]{1,0:T(8,128)(2,1)S(1)}, bf16[32,512]{1,0:T(8,128)(2,1)}, u32[]{:S(2)}) copy-start(bf16[32,512]{1,0:T(8,128)(2,1)} %constant.66.clone.rim_ref) | copy-start | bytes 98308
  0.6 128.3 %copy-start.2 = (bf16[256,256]{1,0:T(8,128)(2,1)S(1)}, bf16[256,256]{1,0:T(8,128)(2,1)}, u32[]{:S(2)}) copy-start(bf16[256,256]{1,0:T(8,128)(2,1)} %constant.65.clone.kl_ref) | copy-start | bytes 393220
  0.7 128.3 %copy-start.3 = (bf16[256,256]{1,0:T(8,128)(2,1)S(1)}, bf16[256,256]{1,0:T(8,128)(2,1)}, u32[]{:S(2)}) copy-start(bf16[256,256]{1,0:T(8,128)(2,1)} %constant.64.clone.ky_ref) | copy-start | bytes 393220
  0.7 128.3 %copy-start.4 = (bf16[256,144]{1,0:T(8,128)(2,1)S(1)}, bf16[256,144]{1,0:T(8,128)(2,1)}, u32[]{:S(2)}) copy-start(bf16[256,144]{1,0:T(8,128)(2,1)} %constant.63.clone.kx_ref) | copy-start | bytes 221188
  9.1 21.5 %all-to-all-start = ((f32[128,1,256]{2,1,0:T(1,128)}), f32[128,1,256]{2,1,0:T(1,128)S(1)}, u32[]{:S(2)}, u32[]{:S(2)}) async-start(f32[128,1,256]{2,1,0:T(1,128)} %copy.22), calls=%async_computation | async-start | bytes 262144 | tf_op jit(solution)/shard_map/all_to_all | solution.py:600
  129.0 1.0 copy-start
  130.0 0.9 copy-start.1

commit v2 on v1

v2 whole, which is shorter than its diff:
```python
import functools
import math

import jax
import jax.numpy as jnp
import numpy as np
from jax import lax
from jax.experimental import pallas as pl
from jax.experimental.pallas import tpu as pltpu
from jax.sharding import PartitionSpec as P

SLOTS = 32
HALF = 0.5
GROUP = 42
BASES = 39
OFF = 8
XEXT = 144
PAIRS = 10
EACH = 8
TILES = 7
COPIES = 2
ROOT = (math.sqrt(5.0) - 3.0) / 2.0
MESH = pl.DeviceIdType.MESH
VMEM = pltpu.VMEM
F32 = jnp.float32
BF16 = jnp.bfloat16


SCALE = 1.0 / (1.0 + 2.0 * ROOT / 3.0)
LEAD = SCALE * (7.0 / 9.0 * (1.0 / ROOT - ROOT) + 1.0 / 36.0 * (1.0 / ROOT**2 - ROOT**2))
NEAR = SCALE / 36.0 * (ROOT - 1.0 / ROOT)


def line_matrix(n):
    gap = np.arange(n)[None, :] - np.arange(n)[:, None]
    out = np.sign(gap) * LEAD * ROOT ** np.abs(gap).astype(np.float64)
    return out + np.where(np.abs(gap) == 1, np.sign(gap) * NEAR, 0.0)


def halo_columns(n):
    out = np.zeros((n, 4))
    steps = np.arange(n)
    out[:, 0] = -LEAD * ROOT ** (steps + 1.0)
    out[0, 1] = -NEAR
    out[:, 2] = LEAD * ROOT ** (n - steps * 1.0)
    out[n - 1, 3] = NEAR
    return out


def halves(values):
    values = np.asarray(values, np.float32)
    high = values.astype(BF16)
    low = (values - high.astype(np.float32)).astype(BF16)
    return high, low


def split(x):
    high = x.astype(BF16)
    return high, (x - high.astype(F32)).astype(BF16)


def dot(a, b):
    return jnp.dot(a, b, preferred_element_type=F32)


def edge_weights(n, total):
    out = np.zeros((8, total))
    steps = np.arange(n)
    out[0, :n] = ROOT ** (n - 1.0 - steps)
    out[1, n - 1] = 1.0
    out[2, n] = 1.0
    out[3, n + 1] = 1.0
    out[4, :n] = ROOT ** (steps * 1.0)
    out[5, 0] = 1.0
    out[6, n + 2] = 1.0
    return out


def pack_kernel(counts_ref, force_ref, frac_ref, cx_ref, cy_ref, cz_ref, out_ref, wide):
    size = force_ref.shape[1]
    wide[0:3, 0:size] = force_ref[...]
    wide[3:6, 0:size] = frac_ref[...]
    code = ((cx_ref[...] * 256 + cy_ref[...]) * 16 + cz_ref[...]).astype(F32)
    for i in range(size // 128):
        wide[6:7, i * 128 : (i + 1) * 128] = code[i : i + 1]
    wide[7:8, 0:size] = jnp.zeros((1, size), F32)
    wide[:, size:] = jnp.zeros((8, wide.shape[1] - size), F32)
    lane = lax.broadcasted_iota(jnp.int32, (8, 128), 1)
    sub = lax.broadcasted_iota(jnp.int32, (8, 128), 0)
    part = sub & 3

    def one(d, start):
        count = counts_ref[0, d]
        first = pl.multiple_of((start >> 7) << 7, 128)
        shift = start & 127
        back = (128 - shift) & 127
        a = pltpu.roll(wide[:, pl.ds(first, 128)], back, 1)
        b = pltpu.roll(wide[:, pl.ds(first + 128, 128)], back, 1)
        w = jnp.where(lane + shift < 128, a, b)
        w = jnp.where(lane < count, w, 0.0)
        m = w
        for j in range(1, 4):
            m = jnp.where(part == j, pltpu.roll(w, SLOTS * j, 1), m)
        top = jnp.sum(jnp.where(sub < 4, m, 0.0), axis=0, keepdims=True)
        low = jnp.sum(jnp.where(sub < 4, 0.0, m), axis=0, keepdims=True)
        return start + count, jnp.concatenate([top, low], axis=1)

    def eight(g, start):
        for k in range(8):
            start, out_ref[k, g] = one(g * 8 + k, start)
        return start

    lax.fori_loop(0, out_ref.shape[1], eight, jnp.int32(0))


def pack(counts, *fields):
    vm = pl.BlockSpec(memory_space=VMEM)
    return pl.pallas_call(
        pack_kernel,
        out_shape=jax.ShapeDtypeStruct((8, counts.shape[1] // 8, 1, 256), F32),
        in_specs=[pl.BlockSpec(memory_space=pltpu.SMEM)] + [vm] * 5,
        out_specs=vm,
        scratch_shapes=[VMEM((8, fields[0].shape[1] + 256), F32)],
        name="pack",
    )(counts, *fields)


def shuffle_kernel(out_ref, in_ref, mid, own_sems, send_y, recv_y, send_x, recv_x):
    gx, gy = lax.axis_index("gx"), lax.axis_index("gy")
    nx, ny = lax.axis_size("gx"), lax.axis_size("gy")
    own = pltpu.make_async_copy(out_ref.at[gy], mid.at[gy], own_sems.at[0])
    own.start()
    barrier = pltpu.get_barrier_semaphore()
    for k in range(1, ny):
        pl.semaphore_signal(barrier, inc=1, device_id=(gx, lax.rem(gy + k, ny)), device_id_type=MESH)
    for k in range(1, nx):
        pl.semaphore_signal(barrier, inc=1, device_id=(lax.rem(gx + k, nx), gy), device_id_type=MESH)
    pl.semaphore_wait(barrier, nx + ny - 2)
    copies = []
    for k in range(1, ny):
        peer = lax.rem(gy + k, ny)
        copy = pltpu.make_async_remote_copy(
            src_ref=out_ref.at[peer], dst_ref=mid.at[gy], send_sem=send_y.at[k], recv_sem=recv_y.at[k],
            device_id=(gx, peer), device_id_type=MESH,
        )
        copy.start()
        copies.append(copy)
    own.wait()
    for copy in copies:
        copy.wait()
    own = pltpu.make_async_copy(mid.at[:, gx], in_ref.at[gx], own_sems.at[1])
    own.start()
    copies = []
    for k in range(1, nx):
        peer = lax.rem(gx + k, nx)
        copy = pltpu.make_async_remote_copy(
            src_ref=mid.at[:, peer], dst_ref=in_ref.at[gx], send_sem=send_x.at[k], recv_sem=recv_x.at[k],
            device_id=(peer, gy), device_id_type=MESH,
        )
        copy.start()
        copies.append(copy)
    own.wait()
    for copy in copies:
        copy.wait()


def shuffle(outbox):
    ny, nx = outbox.shape[0:2]
    anywhere = pl.BlockSpec(memory_space=pl.ANY)
    dma = pltpu.SemaphoreType.DMA
    return pl.pallas_call(
        shuffle_kernel,
        out_shape=jax.ShapeDtypeStruct((nx, ny, 1, 256), F32),
        in_specs=[anywhere],
        out_specs=anywhere,
        scratch_shapes=[VMEM((ny, nx, 1, 256), F32), dma((2,)), dma((ny,)), dma((ny,)), dma((nx,)), dma((nx,))],
        compiler_params=pltpu.CompilerParams(collective_id=1, has_side_effects=True),
        name="shuffle",
    )(outbox)


def row_as_column(row):
    return jnp.transpose(jnp.broadcast_to(row, (128, 128)))


def stencil_weights(t):
    root = jnp.sqrt(jnp.maximum(1.0 + 4.0 * t - 4.0 * t * t, 0.0))
    return (
        (3.0 - 2.0 * t - root) / 8.0,
        (3.0 - 2.0 * t + root) / 8.0,
        (1.0 + 2.0 * t + root) / 8.0,
        (1.0 + 2.0 * t - root) / 8.0,
    )


def spread_kernel(
    inbox_ref, mx_ref, my_ref, pick_ref, tail_ref, wfar_ref, wnear_ref, v_hbm,
    e_hbm, rl_ref, cn_ref, ud_ref,
    *scratch,
):
    grids = scratch[:COPIES]
    vbuf, m8, base_v, base_s, fcy, mxcol, ext, rlp, udp, v_sem, e_sems, s_sem = scratch[COPIES:]
    gx, gy = lax.axis_index("gx"), lax.axis_index("gy")
    chunks = inbox_ref.shape[0] * SLOTS // 128
    vin = pltpu.make_async_copy(v_hbm, vbuf, v_sem)
    vin.start()
    lane = lax.broadcasted_iota(jnp.int32, (8, 128), 1)
    sub = lax.broadcasted_iota(jnp.int32, (8, 128), 0)

    def regroup(g, carry):
        out = None
        for k in range(4):
            row = inbox_ref[g * 4 + k]
            x = jnp.where(
                sub < 4, jnp.broadcast_to(row[:, 0:128], (8, 128)), jnp.broadcast_to(row[:, 128:256], (8, 128))
            )
            y = x
            for j in range(4):
                turn = (SLOTS * (k - j)) % 128
                z = pltpu.roll(x, turn, 1) if turn else x
                y = jnp.where((sub & 3) == j, z, y)
            out = y if out is None else jnp.where((lane >> 5) == k, y, out)
        at = pl.multiple_of(g * 128, 128)
        m8[:, pl.ds(at, 128)] = out
        code = out[6:7].astype(jnp.int32)
        tile = (((code >> 4) & 255) * 1681) >> 16
        base_v[:, pl.ds(at, 128)] = (tile * PAIRS + ((code & 15) >> 1)) * (2 * XEXT) + 2 * ((code >> 12) + OFF - 1)
        return carry

    lax.fori_loop(0, chunks, regroup, 0)
    bcopy = pltpu.make_async_copy(base_v, base_s, s_sem)
    bcopy.start()
    rows = grids[0].shape[0]
    step = 160

    def clear(i, carry):
        for grid in grids:
            grid[pl.ds(pl.multiple_of(i * step, 8), step), :] = jnp.zeros((step, 128), F32)
        return carry

    lax.fori_loop(0, rows // step, clear, 0)
    bcopy.wait()

    sub2 = lax.broadcasted_iota(jnp.int32, (128, 128), 0)
    comp = jnp.where(sub2 >= 2 * GROUP, 2, jnp.where(sub2 >= GROUP, 1, 0))
    rel = jnp.where(sub2 >= 3 * GROUP, -100, sub2 - GROUP * comp)

    def chunk(c, carry):
        m = m8[:, pl.ds(pl.multiple_of(c * 128, 128), 128)]
        ws = stencil_weights(m)
        code = m[6:7].astype(jnp.int32)
        cell_y = (code >> 4) & 255
        inner = cell_y - BASES * ((cell_y * 1681) >> 16)
        d = rel - inner
        w = jnp.where(d == 0, ws[0][4:5], 0.0)
        w = jnp.where(d == 1, ws[1][4:5], w)
        w = jnp.where(d == 2, ws[2][4:5], w)
        w = jnp.where(d == 3, ws[3][4:5], w)
        f = jnp.where(comp == 0, m[0:1], jnp.where(comp == 1, m[1:2], m[2:3]))
        fcy[...] = jnp.transpose(w * f)
        odd = (code & 1) == 1
        wx = [w[3:4] for w in ws]
        wz = [w[5:6] for w in ws]
        none = jnp.zeros((1, 128), F32)
        sides = (
            (jnp.where(odd, none, wz[0]), jnp.where(odd, wz[0], wz[1])),
            (jnp.where(odd, wz[1], wz[2]), jnp.where(odd, wz[2], wz[3])),
            (jnp.where(odd, wz[3], none), none),
        )
        wx8 = jnp.concatenate([wx[i // 2] for i in range(8)], axis=0)
        tall = [wx8 * jnp.concatenate(list(side) * 4, axis=0) for side in sides]
        fr = fcy[...]
        bs = [base_s[0, c * 128 + k] for k in range(128)]
        for k0 in range(0, 128, COPIES):
            group = []
            for k in range(k0, k0 + COPIES):
                grid = grids[k % COPIES]
                for q in range(3):
                    at = bs[k] + q * (2 * XEXT)
                    group.append((grid, at, grid[pl.ds(at, 8), :] + tall[q][:, k : k + 1] * fr[k : k + 1, :]))
            for grid, at, value in group:
                grid[pl.ds(at, 8), :] = value
        return carry

    lax.fori_loop(0, chunks, chunk, 0)

    def first_row(t, e):
        return (t * PAIRS + (e >> 1)) * (2 * XEXT) + (e & 1)

    for t in range(TILES):
        for src, dst in ((0, 16), (17, 1), (18, 2)):
            moved = None
            for grid in grids:
                x = grid[pl.ds(first_row(t, src), XEXT, stride=2), :]
                moved = x if moved is None else moved + x
            here = pl.ds(first_row(t, dst), XEXT, stride=2)
            grids[0][here, :] = grids[0][here, :] + moved

    nx, ny = mx_ref.shape[0], my_ref.shape[0]
    mxcol[0:OFF, :] = row_as_column(mx_ref[pl.ds(lax.rem(gx + nx - 1, nx), 1), :])[128 - OFF : 128]
    mxcol[OFF : OFF + 128, :] = row_as_column(mx_ref[pl.ds(gx, 1), :])
    mxcol[OFF + 128 : XEXT, :] = row_as_column(mx_ref[pl.ds(lax.rem(gx + 1, nx), 1), :])[0 : XEXT - OFF - 128]
    after = my_ref[pl.ds(lax.rem(2 * gy + 2, ny), 1), :]
    before = pltpu.roll(jnp.broadcast_to(my_ref[pl.ds(lax.rem(2 * gy + ny - 1, ny), 1), :], (8, 128)), 3, 1)[0:1]
    lane1 = lax.broadcasted_iota(jnp.int32, (1, 128), 1)
    rim = jnp.where(lane1 < 2, after, jnp.where(lane1 == 2, before, 0.0))
    mys = [HALF * my_ref[pl.ds(2 * gy, 1), :], HALF * my_ref[pl.ds(2 * gy + 1, 1), :], HALF * rim]
    vin.wait()

    part = 48
    lanes = lax.broadcasted_iota(jnp.int32, (part, 128), 1)

    def moves(c, h):
        out = []
        if h == 2:
            out.append((6, (-(GROUP * c + 256 - (6 * BASES - 1))) % 128, 0, 2))
            out.append((0, (2 - GROUP * c) % 128, 2, 3))
            return out
        for t in range(TILES):
            low, high = BASES * t - 1 - 128 * h, BASES * t - 1 + GROUP - 128 * h
            if high > 0 and low < 128:
                out.append((t, (low - GROUP * c) % 128, max(low, 0), min(high, 128)))
        return out

    def plane(z, carry):
        far = [[jnp.zeros((8, 128), F32)] * 3 for _ in range(3)]
        near = [[jnp.zeros((8, 128), F32)] * 3 for _ in range(3)]
        for r0 in range(0, XEXT, part):
            tiles = []
            for t in range(TILES):
                x = None
                for grid in grids:
                    y = grid[pl.ds(first_row(t, z + 1) + 2 * r0, part, stride=2), :]
                    x = y if x is None else x + y
                tiles.append(x)
            mcol = mxcol[r0 : r0 + part, :]
            wf, wn = wfar_ref[r0 : r0 + part, :], wnear_ref[r0 : r0 + part, :]
            r1 = r0 + part
            i0, i1 = max(r0, OFF), min(r1, OFF + 128)
            for c in range(3):
                for h in range(3):
                    e = None
                    for t, turn, low, high in moves(c, h):
                        x = pltpu.roll(tiles[t], turn, 1) if turn else tiles[t]
                        if low > 0 or high < 128:
                            x = jnp.where((lanes >= low) & (lanes < high), x, 0.0)
                        e = x if e is None else e + x
                    e = e * mcol * mys[h]
                    if h < 2:
                        cols = slice(h * 128, (h + 1) * 128)
                        inner = e[i0 - r0 : i1 - r0] + vbuf[c, z, i0 - OFF : i1 - OFF, cols]
                        vbuf[c, z, i0 - OFF : i1 - OFF, cols] = inner
                        pieces = [e[0 : i0 - r0]] if i0 > r0 else []
                        pieces.append(inner)
                        if i1 < r1:
                            pieces.append(e[i1 - r0 :])
                        e = jnp.concatenate(pieces, axis=0) if len(pieces) > 1 else inner
                    ext[c, h, r0:r1, :] = e
                    far[c][h] = far[c][h] + jnp.sum((e * wf).reshape(part // 8, 8, 128), axis=0)
                    near[c][h] = near[c][h] + jnp.sum((e * wn).reshape(part // 8, 8, 128), axis=0)
        for c in range(3):
            p = c * 16 + z
            at = pl.multiple_of(p * 8, 8)
            for h in range(3):
                rowset = [
                    jnp.sum(far[c][h], axis=0, keepdims=True),
                    ext[c, h, OFF + 127 : OFF + 130, :],
                    jnp.sum(near[c][h], axis=0, keepdims=True),
                    ext[c, h, OFF : OFF + 1, :],
                    ext[c, h, OFF - 1 : OFF, :],
                    jnp.zeros((1, 128), F32),
                ]
                rlp[h, pl.ds(at, 8), :] = jnp.concatenate(rowset, axis=0)
            high, low = split(jnp.concatenate([ext[c, h, OFF : OFF + 128, :] for h in range(3)], axis=1))
            nt = (((1,), (1,)), ((), ()))
            one = lax.dot_general(pick_ref[...], high, nt, preferred_element_type=F32)
            two = lax.dot_general(pick_ref[...], low, nt, preferred_element_type=F32)
            udp[pl.ds(at, 8), :] = one[0:8] + one[8:16] + two[0:8]
        pltpu.make_async_copy(vbuf.at[:, z], e_hbm.at[:, z], e_sems.at[z]).start()
        return carry

    lax.fori_loop(0, 16, plane, 0)

    corner = jnp.zeros((48, 128), F32)
    for t in range(7):
        row = jnp.concatenate([rlp[h, pl.ds(t, 48, stride=8), :] for h in range(3)], axis=1)
        rl_ref[t] = row[:, 0:256]
        ends = jnp.dot(row, tail_ref[...], preferred_element_type=F32, precision=lax.Precision.HIGHEST)
        corner = corner + (pltpu.roll(ends, 8 * t, 1) if t else ends)
        ud_ref[t] = udp[pl.ds(t, 48, stride=8), :]
    rl_ref[7] = jnp.zeros((48, 256), F32)
    ud_ref[7] = jnp.zeros((48, 128), F32)
    cn_ref[...] = corner
    for z in range(16):
        pltpu.make_async_copy(vbuf.at[:, z], e_hbm.at[:, z], e_sems.at[z]).wait()


def spread(inbox, mx, my, v):
    ends = edge_weights(256, 384)
    high, low = halves(ends)
    pick = np.concatenate([high, low], axis=0)
    tail = np.zeros((384, 128), np.float32)
    tail[:, 0:8] = ends.T
    weights = edge_weights(128, 144)
    far = np.zeros((XEXT, 128), np.float32)
    near = np.zeros((XEXT, 128), np.float32)
    far[OFF : OFF + 128] = weights[0, 0:128, None]
    near[OFF : OFF + 128] = weights[4, 0:128, None]
    rows = TILES * PAIRS * 2 * XEXT
    total = inbox.shape[0] * SLOTS
    vm = pl.BlockSpec(memory_space=VMEM)
    return pl.pallas_call(
        spread_kernel,
        out_shape=(
            jax.ShapeDtypeStruct(v.shape, F32),
            jax.ShapeDtypeStruct((8, 48, 256), F32),
            jax.ShapeDtypeStruct((48, 128), F32),
            jax.ShapeDtypeStruct((8, 48, 128), F32),
        ),
        in_specs=[vm] * 7 + [pl.BlockSpec(memory_space=pl.ANY)],
        out_specs=(pl.BlockSpec(memory_space=pl.ANY), vm, vm, vm),
        scratch_shapes=[VMEM((rows, 128), F32)] * COPIES
        + [
            VMEM(v.shape, F32),
            VMEM((8, total), F32),
            VMEM((1, total), jnp.int32),
            pltpu.SMEM((1, total), jnp.int32),
            VMEM((128, 128), F32),
            VMEM((XEXT, 128), F32),
            VMEM((3, 3, XEXT, 128), F32),
            VMEM((3, 48 * 8, 128), F32),
            VMEM((48 * 8, 128), F32),
            pltpu.SemaphoreType.DMA,
            pltpu.SemaphoreType.DMA((16,)),
            pltpu.SemaphoreType.DMA,
        ],
        compiler_params=pltpu.CompilerParams(vmem_limit_bytes=60 << 20),
        name="spread",
    )(inbox, mx, my, pick, tail, far, near, v)


def exchange_kernel(
    rl_hbm, cn_hbm, ud_hbm, xh_ref, yh_ref, rl_ref, cn_ref, ud_ref,
    ra, ca, rb, cb, umsg, hmsg, pu, ph, qd, qh, own_sems, send_sems, recv_sems,
):
    pairs = ((cn_hbm, cn_ref), (ud_hbm, ud_ref), (rl_hbm, rl_ref))
    loads = [pltpu.make_async_copy(src, dst, own_sems.at[i]) for i, (src, dst) in enumerate(pairs)]
    for load in loads:
        load.start()
    gx, gy = lax.axis_index("gx"), lax.axis_index("gy")
    nx, ny = lax.axis_size("gx"), lax.axis_size("gy")
    right = (lax.rem(gx + 1, nx), gy)
    left = (lax.rem(gx + nx - 1, nx), gy)
    up = (gx, lax.rem(gy + 1, ny))
    down = (gx, lax.rem(gy + ny - 1, ny))
    barrier = pltpu.get_barrier_semaphore()
    for device in (right, left, up, down):
        pl.semaphore_signal(barrier, inc=1, device_id=device, device_id_type=MESH)
    pl.semaphore_wait(barrier, 4)

    def send(i, src, dst, device):
        copy = pltpu.make_async_remote_copy(
            src_ref=src, dst_ref=dst, send_sem=send_sems.at[i], recv_sem=recv_sems.at[i],
            device_id=device, device_id_type=MESH,
        )
        copy.start()
        return copy

    first = [
        send(0, cn_hbm, ca, right),
        send(1, cn_hbm, cb, left),
        send(2, rl_hbm.at[0:4], ra, right),
        send(3, rl_hbm.at[4:7], rb, left),
    ]
    planes = cn_ref.shape[0]
    lane = lax.broadcasted_iota(jnp.int32, (planes, 128), 1)
    for load in loads:
        load.wait()
    first[0].wait()
    first[1].wait()
    own, a, b = cn_ref[...], ca[...], cb[...]
    turn = lambda x, by: pltpu.roll(x, by % 128, 1)
    hold = jnp.where(lane < 8, a + turn(own, -48), a + turn(own, -40))
    hold = jnp.where(
        lane < 16, hold, turn(b, -16) + jnp.where(lane < 24, own + ROOT * turn(own, -8), turn(own, 8))
    )
    hmsg[...] = jnp.where(lane < 32, hold, 0.0)
    for s in range(7):
        umsg[s] = (
            ud_ref[s]
            + jnp.where(lane == 0, a[:, 16 + s : 17 + s], 0.0)
            + jnp.where(lane == 1, a[:, 24 + s : 25 + s], 0.0)
            + jnp.where(lane == 127, b[:, 48 + s : 49 + s], 0.0)
        )
    second = [
        send(4, hmsg, ph, up),
        send(5, hmsg, qh, down),
        send(6, umsg.at[0:4], pu, up),
        send(7, umsg.at[4:7], qd, down),
    ]
    first[2].wait()
    first[3].wait()
    second[0].wait()
    second[1].wait()
    lane = lax.broadcasted_iota(jnp.int32, (planes, 256), 1)
    p, q = ph[...], qh[...]

    def rims(h):
        return (
            jnp.where(lane == 0, p[:, 8 * h + 2 : 8 * h + 3], 0.0)
            + jnp.where(lane == 1, p[:, 8 * h + 3 : 8 * h + 4], 0.0)
            + jnp.where(lane == 255, q[:, 8 * h + 6 : 8 * h + 7], 0.0)
        )

    def put(t, value):
        for h in range(2):
            xh_ref[h, pl.ds(t, planes, stride=8), :] = value[:, h * 128 : (h + 1) * 128]

    put(0, ra[0] + rl_ref[6] + rims(0))
    put(1, ra[1] + rl_ref[6] + rims(1))
    put(2, rb[0] + rl_ref[2] + ROOT * rl_ref[3] + rims(2))
    put(3, rb[1] + rl_ref[2] + rims(3))
    put(4, ra[2])
    put(5, ra[3])
    put(6, rb[2])
    put(7, jnp.zeros((planes, 256), F32))
    second[2].wait()
    second[3].wait()
    yh_ref[pl.ds(0, planes, stride=8), :] = pu[0] + umsg[6]
    yh_ref[pl.ds(1, planes, stride=8), :] = pu[1] + umsg[6]
    yh_ref[pl.ds(2, planes, stride=8), :] = qd[0] + umsg[2] + ROOT * umsg[3]
    yh_ref[pl.ds(3, planes, stride=8), :] = qd[1] + umsg[2]
    yh_ref[pl.ds(4, planes, stride=8), :] = pu[2]
    yh_ref[pl.ds(5, planes, stride=8), :] = pu[3]
    yh_ref[pl.ds(6, planes, stride=8), :] = qd[2]
    yh_ref[pl.ds(7, planes, stride=8), :] = jnp.zeros((planes, 128), F32)


def exchange(rl, cn, ud):
    n = cn.shape[0]
    vm = pl.BlockSpec(memory_space=VMEM)
    return pl.pallas_call(
        exchange_kernel,
        out_shape=(jax.ShapeDtypeStruct((2, 8 * n, 128), F32), jax.ShapeDtypeStruct((8 * n, 128), F32)),
        in_specs=[pl.BlockSpec(memory_space=pl.ANY)] * 3,
        out_specs=(vm, vm),
        scratch_shapes=[
            VMEM((8, n, 256), F32),
            VMEM((n, 128), F32),
            VMEM((8, n, 128), F32),
            VMEM((4, n, 256), F32),
            VMEM((n, 128), F32),
            VMEM((3, n, 256), F32),
            VMEM((n, 128), F32),
            VMEM((7, n, 128), F32),
            VMEM((n, 128), F32),
            VMEM((4, n, 128), F32),
            VMEM((n, 128), F32),
            VMEM((3, n, 128), F32),
            VMEM((n, 128), F32),
            pltpu.SemaphoreType.DMA((3,)),
            pltpu.SemaphoreType.DMA((8,)),
            pltpu.SemaphoreType.DMA((8,)),
        ],
        compiler_params=pltpu.CompilerParams(collective_id=0, has_side_effects=True),
        name="exchange",
    )(rl, cn, ud)


def derive_kernel(e_ref, xh_ref, yh_ref, mx_ref, my_ref, kx_ref, ky_ref, kl_ref, rim_ref, dx_ref, dy_ref, mxcol, myrow):
    @pl.when(pl.program_id(0) == 0)
    def _():
        gx, gy = lax.axis_index("gx"), lax.axis_index("gy")
        mxcol[...] = row_as_column(mx_ref[pl.ds(gx, 1), :])
        myrow[:, 0:128] = jnp.broadcast_to(my_ref[pl.ds(2 * gy, 1), :], (8, 128))
        myrow[:, 128:256] = jnp.broadcast_to(my_ref[pl.ds(2 * gy + 1, 1), :], (8, 128))

    each = e_ref.shape[0]
    zero = jnp.zeros((1, 256), F32)
    col = mxcol[...]
    yall = jnp.concatenate([yh_ref[i * 8 : i * 8 + 8, :] for i in range(each)], axis=1)
    high = yall.astype(BF16).astype(F32)
    stack = jnp.concatenate([high, yall - high, high, jnp.zeros_like(high)], axis=0).astype(BF16)
    extra = lax.dot_general(stack, rim_ref[...], (((0,), (0,)), ((), ())), preferred_element_type=F32)
    highs, lows = [], []
    for i in range(each):
        xall = jnp.concatenate([xh_ref[0, i * 8 : i * 8 + 8, :], xh_ref[1, i * 8 : i * 8 + 8, :]], axis=1)
        top = jnp.concatenate([xall[4:6]] + [zero] * 6, axis=0)
        low = jnp.concatenate([zero] * 7 + [xall[6:7]], axis=0)
        e = e_ref[i]
        f = jnp.concatenate([e[0:8] + top, e[8:120], e[120:128] + low], axis=0)
        f = f + extra[i * 128 : (i + 1) * 128, 256:512]
        halo = jnp.concatenate([xall[0:4]] + [zero] * 12, axis=0)
        fh, fl = split(f)
        hh, hl = split(halo)
        highs.append(fh)
        lows.append(fl)
        one = dot(kx_ref[...], jnp.concatenate([fh, hh], axis=0))
        dx = one[0:128] + one[128:256] + dot(kx_ref[0:128], jnp.concatenate([fl, hl], axis=0))
        dx_ref[i, :, 0:128] = dx[:, 0:128] * col
        dx_ref[i, :, 128:256] = dx[:, 128:256] * col
    two = dot(jnp.concatenate(highs + lows, axis=0), ky_ref[...])
    n = each * 128
    dy = two[0:n] + two[n : 2 * n] + dot(jnp.concatenate(highs, axis=0), kl_ref[...]) + extra[:, 0:256]
    dy_ref[...] = (dy * myrow[0:1, :]).reshape(dy_ref.shape)


def derive(e, xh, yh, mx, my):
    n, rows, cols = e.shape
    each = EACH
    kx = np.zeros((rows, 144))
    kx[:, 0:rows] = line_matrix(rows)
    kx[:, rows : rows + 4] = halo_columns(rows)
    kx = np.concatenate(halves(kx), axis=0)
    kh, kl = halves(line_matrix(cols).T)
    rim = np.zeros((8, 512))
    rim[0:4, 0:256] = halo_columns(cols).T
    rim[4, 256] = 1.0
    rim[5, 257] = 1.0
    rim[6, 511] = 1.0
    rh, rlow = halves(rim)
    rim = np.concatenate([rh, rh, rlow, np.zeros((8, 512), BF16)], axis=0)
    whole = lambda x: pl.BlockSpec(x.shape, lambda i: (0,) * x.ndim)
    block = pl.BlockSpec((each, rows, cols), lambda i: (i, 0, 0))
    consts = (kx, kh, kl, rim)
    xspec = pl.BlockSpec((2, each * 8, 128), lambda i: (0, i, 0))
    yspec = pl.BlockSpec((each * 8, 128), lambda i: (i, 0))
    return pl.pallas_call(
        derive_kernel,
        grid=(n // each,),
        out_shape=(jax.ShapeDtypeStruct(e.shape, F32),) * 2,
        in_specs=[block, xspec, yspec] + [whole(x) for x in (mx, my) + consts],
        out_specs=(block, block),
        scratch_shapes=[VMEM((128, 128), F32), VMEM((8, 256), F32)],
        compiler_params=pltpu.CompilerParams(vmem_limit_bytes=62 << 20),
        name="derive",
    )(e, xh, yh, mx, my, *consts)


def local(
    velocity, metric_x, metric_y, marker_force, marker_frac, marker_cell_x, marker_cell_y, marker_cell_z, send_counts
):
    comps, planes, rows, cols = velocity.shape
    fold = lambda x: x.reshape(-1, 128)
    cells = [fold(x) for x in (marker_cell_x, marker_cell_y, marker_cell_z)]
    outbox = pack(send_counts, marker_force, marker_frac, *cells)
    inbox = shuffle(outbox).reshape(-1, 1, 256)
    mx, my = fold(metric_x), fold(metric_y)
    e, rl, cn, ud = spread(inbox, mx, my, velocity)
    xh, yh = exchange(rl, cn, ud)
    dx, dy = derive(e.reshape(comps * planes, rows, cols), xh, yh, mx, my)
    return dx.reshape(velocity.shape), dy.reshape(velocity.shape)


def solution(mesh):
    both = ("gx", "gy")
    placed = (
        P(None, None, "gx", "gy"), P(), P(), P(None, both), P(None, both), P(both), P(both), P(both), P(both, None),
    )
    return jax.shard_map(
        local,
        mesh=mesh,
        in_specs=placed,
        out_specs=(P(None, None, "gx", "gy"), P(None, None, "gx", "gy")),
        check_vma=False,
    )
```

time: 148 us -> 88.4 us (0.60)
  Pallas kernels: 117 us -> 87.4 us
  local copies, waits for them, and re-layouts: 13.4 us -> 0 us
  starting transfers between devices: 11.5 us -> 0 us
  other arithmetic: 3.01 us -> 0 us
    pallas_call x1, Pallas kernels: 83 us -> 42.3 us  [spread(): pl.pallas_call(spread_kernel, out_shape=(jax.ShapeDtypeStruct(v.shape, F3...]
    pallas_call x1 -> x2, Pallas kernels: 4.33 us -> 21.3 us  [the longest x1 16.9 us: shuffle(): pl.pallas_call(shuffle_kernel, out_shape=jax.ShapeDtypeStruct((nx, ny, 1,...]
    all_to_all x1 -> x0, starting transfers between devices: 11.5 us -> none  [local(): lax.all_to_all(outbox, ('gx', 'gy'), split_axis=0, concat_axis=0, tiled=T...]
    pallas_call x1, Pallas kernels: 15.9 us -> 11 us  [derive(): pl.pallas_call(derive_kernel, grid=(n // each,), out_shape=(jax.ShapeDtyp...]
    slice x4 -> x0, local copies, waits for them, and re-layouts: 3.4 us -> none  [the longest x2 1.96 us: metrics(): long = jnp.concatenate([metric_y[ny - 1:], metric_y, metric_y[:2]])]
    unnamed x13 -> x0, local copies, waits for them, and re-layouts: 2.6 us -> none
    concatenate x3 -> x0, local copies, waits for them, and re-layouts: 2.27 us -> none  [the longest x1 1.42 us: metrics(): long = jnp.concatenate([metric_y[ny - 1:], metric_y, metric_y[:2]])]
    dynamic_slice x5 -> x0, local copies, waits for them, and re-layouts: 2.25 us -> none  [the longest x1 0.76 us: metrics(): inner = lax.dynamic_slice(metric_y, (gy * cols,), (cols,))]
  transfers between devices with their start and end apart: 1 -> 0, of which waited for: 1 -> 0; matrix products, arithmetic and copies ran while one was open for 6% -> 0% of each run, Pallas kernels for 0% -> 0%
where the time goes in v2:
time: 88.4 us; the launch traced here: 88 us
  Pallas kernels  87.4 us (99%)
    pallas_call x1, Pallas kernels, spread(): pl.pallas_call(spread_kernel, out_shape=(jax.ShapeDtypeStruct(v.shape, F3...  42.3 us
    pallas_call x1, Pallas kernels, shuffle(): pl.pallas_call(shuffle_kernel, out_shape=jax.ShapeDtypeStruct((nx, ny, 1,...  16.9 us
    pallas_call x1, Pallas kernels, exchange(): pl.pallas_call(exchange_kernel, out_shape=(jax.ShapeDtypeStruct((2, 8 * n...  12.8 us
    pallas_call x1, Pallas kernels, derive(): pl.pallas_call(derive_kernel, grid=(n // each,), out_shape=(jax.ShapeDtyp...  11 us
    pallas_call x1, Pallas kernels, pack(): pl.pallas_call(pack_kernel, out_shape=jax.ShapeDtypeStruct((8, counts.sha...  4.37 us

profile of v2, /device:TPU:1, one launch (start us, length us, event | category | flops | bytes accessed | tf_op | source)
XLA Modules:
  0.0 88.0 jit_solution(12002301584242155843)
XLA Ops:
  0.6 4.4 %pack.1.out_ref = f32[8,16,1,256]{3,2,1,0:T(1,128)} custom-call(s32[1,128]{1,0:T(1,128)} %counts_ref.1, f32[3,2048]{1,0:T(4,128)} %force_ref.1, f32[3,2048]{1,0:T(4,128)} %frac_ref.1, s32[16,128]{1,0:T(8,128)} %bitcast.15, s32[16,128]{1,0:T(8,128)} %bitcast.16, s32[16,128]{1,0:T(8,128)} %bitcast.17), custom_call_target="tpu_custom_call" | custom-call | tf_op jit(solution)/shard_map/pack/pallas_call | solution.py:118
  5.0 16.9 %shuffle.1 = f32[16,8,1,256]{3,2,1,0:T(1,128)} custom-call(f32[8,16,1,256]{3,2,1,0:T(1,128)} %pack.1.out_ref), custom_call_target="tpu_custom_call" | custom-call | tf_op jit(solution)/shard_map/shuffle/pallas_call | solution.py:171
  22.0 42.3 %spread.1 = (f32[3,16,128,256]{3,2,1,0:T(8,128)}, f32[8,48,256]{2,1,0:T(8,128)}, f32[48,128]{1,0:T(8,128)}, f32[8,48,128]{2,1,0:T(8,128)}) custom-call(f32[128,1,256]{2,1,0:T(1,128)} %bitcast.10, f32[16,128]{1,0:T(8,128)} %bitcast.11, f32[16,128]{1,0:T(8,128)} %bitcast.13, bf16[16,384]{1,0:T(8,128)(2,1)} %constant.16.clone.pick_ref, ...), custom_call_target="tpu_custom_call" | custom-call | tf_op jit(solution)/shard_map/spread/pallas_call | solution.py:412
  64.2 12.8 %exchange.1 = (f32[2,384,128]{2,1,0:T(8,128)}, f32[384,128]{1,0:T(8,128)}) custom-call(f32[8,48,256]{2,1,0:T(8,128)} %get-tuple-element.11.rl_hbm, f32[48,128]{1,0:T(8,128)} %get-tuple-element.12.cn_hbm, f32[8,48,128]{2,1,0:T(8,128)} %get-tuple-element.13.ud_hbm), custom_call_target="tpu_custom_call" | custom-call | tf_op jit(solution)/shard_map/exchange/pallas_call | solution.py:542
  77.0 11.0 %derive.1 = (f32[48,128,256]{2,1,0:T(8,128)}, f32[48,128,256]{2,1,0:T(8,128)}) custom-call(f32[48,128,256]{2,1,0:T(8,128)} %bitcast.9, f32[2,384,128]{2,1,0:T(8,128)} %get-tuple-element.14.xh_ref, f32[384,128]{1,0:T(8,128)} %get-tuple-element.15.yh_ref, f32[16,128]{1,0:T(8,128)} %bitcast.12, f32[16,128]{1,0:T(8,128)} %bitcast.14, ...), custom_call_target="tpu_custom_call" | custom-call | tf_op jit(solution)/shard_map/derive/pallas_call | solution.py:628

commit v3 on v2

--- a/solution.py
+++ b/solution.py
@@ -15,7 +15,8 @@
 BASES = 39
 OFF = 8
 XEXT = 144
-PAIRS = 10
+PAIRS = 9
+SPAN = 2 * XEXT
 EACH = 8
 TILES = 7
 COPIES = 2
@@ -63,17 +64,8 @@
     return jnp.dot(a, b, preferred_element_type=F32)
 
 
-def edge_weights(n, total):
-    out = np.zeros((8, total))
-    steps = np.arange(n)
-    out[0, :n] = ROOT ** (n - 1.0 - steps)
-    out[1, n - 1] = 1.0
-    out[2, n] = 1.0
-    out[3, n + 1] = 1.0
-    out[4, :n] = ROOT ** (steps * 1.0)
-    out[5, 0] = 1.0
-    out[6, n + 2] = 1.0
-    return out
+def cost(size):
+    return pl.CostEstimate(flops=0, bytes_accessed=size, transcendentals=0)
 
 
 def pack_kernel(counts_ref, force_ref, frac_ref, cx_ref, cy_ref, cz_ref, out_ref, wide):
@@ -121,6 +113,7 @@
         in_specs=[pl.BlockSpec(memory_space=pltpu.SMEM)] + [vm] * 5,
         out_specs=vm,
         scratch_shapes=[VMEM((8, fields[0].shape[1] + 256), F32)],
+        cost_estimate=cost(12 << 20),
         name="pack",
     )(counts, *fields)
 
@@ -175,6 +168,7 @@
         out_specs=anywhere,
         scratch_shapes=[VMEM((ny, nx, 1, 256), F32), dma((2,)), dma((ny,)), dma((ny,)), dma((nx,)), dma((nx,))],
         compiler_params=pltpu.CompilerParams(collective_id=1, has_side_effects=True),
+        cost_estimate=cost(36 << 20),
         name="shuffle",
     )(outbox)
 
@@ -193,13 +187,27 @@
     )
 
 
+def powers(steps):
+    size = jnp.exp(steps.astype(F32) * math.log(-ROOT))
+    return jnp.where((steps & 1) == 1, -size, size)
+
+
+def edge_table(n, kinds, spots):
+    inside = (spots >= 0) & (spots < n)
+    steps = jnp.where(kinds == 0, n - 1 - spots, spots)
+    sums = jnp.where(inside & ((kinds == 0) | (kinds == 4)), powers(jnp.where(inside, steps, 0)), 0.0)
+    only = jnp.where(kinds < 4, n - 2 + kinds, jnp.where(kinds == 5, 0, n + 2))
+    single = (kinds != 0) & (kinds != 4) & (kinds < 7) & (spots == only)
+    return jnp.where(single, 1.0, sums)
+
+
 def spread_kernel(
-    inbox_ref, mx_ref, my_ref, pick_ref, tail_ref, wfar_ref, wnear_ref, v_hbm,
+    inbox_ref, mx_ref, my_ref, v_hbm,
     e_hbm, rl_ref, cn_ref, ud_ref,
     *scratch,
 ):
     grids = scratch[:COPIES]
-    vbuf, m8, base_v, base_s, fcy, mxcol, ext, rlp, udp, v_sem, e_sems, s_sem = scratch[COPIES:]
+    vbuf, m8, base_v, base_s, fcy, mxcol, wfar_ref, wnear_ref, pick_ref, ext, rlp, udp, v_sem, e_sems, s_sem = scratch[COPIES:]
     gx, gy = lax.axis_index("gx"), lax.axis_index("gy")
     chunks = inbox_ref.shape[0] * SLOTS // 128
     vin = pltpu.make_async_copy(v_hbm, vbuf, v_sem)
@@ -207,7 +215,7 @@
     lane = lax.broadcasted_iota(jnp.int32, (8, 128), 1)
     sub = lax.broadcasted_iota(jnp.int32, (8, 128), 0)
 
-    def regroup(g, carry):
+    def regroup(g):
         out = None
         for k in range(4):
             row = inbox_ref[g * 4 + k]
@@ -220,25 +228,31 @@
                 z = pltpu.roll(x, turn, 1) if turn else x
                 y = jnp.where((sub & 3) == j, z, y)
             out = y if out is None else jnp.where((lane >> 5) == k, y, out)
-        at = pl.multiple_of(g * 128, 128)
+        at = g * 128 if isinstance(g, int) else pl.multiple_of(g * 128, 128)
         m8[:, pl.ds(at, 128)] = out
         code = out[6:7].astype(jnp.int32)
         tile = (((code >> 4) & 255) * 1681) >> 16
-        base_v[:, pl.ds(at, 128)] = (tile * PAIRS + ((code & 15) >> 1)) * (2 * XEXT) + 2 * ((code >> 12) + OFF - 1)
+        pair = (2 * tile + (code & 1)) * PAIRS + ((code & 15) >> 1)
+        base_v[:, pl.ds(at, 128)] = pair * SPAN + 2 * ((code >> 12) + OFF - 1)
+
+    rows = grids[0].shape[0]
+    share = 8 * (-(-rows // (8 * chunks)))
+    full = rows // share
+
+    def regroup_and_clear(g, carry):
+        for grid in grids:
+            grid[pl.ds(pl.multiple_of(g * share, 8), share), :] = jnp.zeros((share, 128), F32)
+        regroup(g)
         return carry
 
-    lax.fori_loop(0, chunks, regroup, 0)
+    lax.fori_loop(0, full, regroup_and_clear, 0)
+    for grid in grids:
+        if full * share < rows:
+            grid[full * share : rows, :] = jnp.zeros((rows - full * share, 128), F32)
+    for g in range(full, chunks):
+        regroup(g)
     bcopy = pltpu.make_async_copy(base_v, base_s, s_sem)
     bcopy.start()
-    rows = grids[0].shape[0]
-    step = 160
-
-    def clear(i, carry):
-        for grid in grids:
-            grid[pl.ds(pl.multiple_of(i * step, 8), step), :] = jnp.zeros((step, 128), F32)
-        return carry
-
-    lax.fori_loop(0, rows // step, clear, 0)
     bcopy.wait()
 
     sub2 = lax.broadcasted_iota(jnp.int32, (128, 128), 0)
@@ -258,15 +272,9 @@
         w = jnp.where(d == 3, ws[3][4:5], w)
         f = jnp.where(comp == 0, m[0:1], jnp.where(comp == 1, m[1:2], m[2:3]))
         fcy[...] = jnp.transpose(w * f)
-        odd = (code & 1) == 1
         wx = [w[3:4] for w in ws]
         wz = [w[5:6] for w in ws]
-        none = jnp.zeros((1, 128), F32)
-        sides = (
-            (jnp.where(odd, none, wz[0]), jnp.where(odd, wz[0], wz[1])),
-            (jnp.where(odd, wz[1], wz[2]), jnp.where(odd, wz[2], wz[3])),
-            (jnp.where(odd, wz[3], none), none),
-        )
+        sides = ((wz[0], wz[1]), (wz[2], wz[3]))
         wx8 = jnp.concatenate([wx[i // 2] for i in range(8)], axis=0)
         tall = [wx8 * jnp.concatenate(list(side) * 4, axis=0) for side in sides]
         fr = fcy[...]
@@ -275,8 +283,8 @@
             group = []
             for k in range(k0, k0 + COPIES):
                 grid = grids[k % COPIES]
-                for q in range(3):
-                    at = bs[k] + q * (2 * XEXT)
+                for q in range(2):
+                    at = bs[k] + q * SPAN
                     group.append((grid, at, grid[pl.ds(at, 8), :] + tall[q][:, k : k + 1] * fr[k : k + 1, :]))
             for grid, at, value in group:
                 grid[pl.ds(at, 8), :] = value
@@ -284,16 +292,17 @@
 
     lax.fori_loop(0, chunks, chunk, 0)
 
-    def first_row(t, e):
-        return (t * PAIRS + (e >> 1)) * (2 * XEXT) + (e & 1)
+    def spots(t, e, odds=(0, 1)):
+        return [(2 * t + odd) * PAIRS * SPAN + ((e - odd) >> 1) * SPAN + ((e - odd) & 1) for odd in odds]
 
     for t in range(TILES):
-        for src, dst in ((0, 16), (17, 1), (18, 2)):
+        for src, odds, dst in ((0, (0,), 16), (17, (0, 1), 1), (18, (1,), 2)):
             moved = None
             for grid in grids:
-                x = grid[pl.ds(first_row(t, src), XEXT, stride=2), :]
-                moved = x if moved is None else moved + x
-            here = pl.ds(first_row(t, dst), XEXT, stride=2)
+                for at in spots(t, src, odds):
+                    x = grid[pl.ds(at, XEXT, stride=2), :]
+                    moved = x if moved is None else moved + x
+            here = pl.ds(spots(t, dst)[0], XEXT, stride=2)
             grids[0][here, :] = grids[0][here, :] + moved
 
     nx, ny = mx_ref.shape[0], my_ref.shape[0]
@@ -305,6 +314,12 @@
     lane1 = lax.broadcasted_iota(jnp.int32, (1, 128), 1)
     rim = jnp.where(lane1 < 2, after, jnp.where(lane1 == 2, before, 0.0))
     mys = [HALF * my_ref[pl.ds(2 * gy, 1), :], HALF * my_ref[pl.ds(2 * gy + 1, 1), :], HALF * rim]
+    at = lax.broadcasted_iota(jnp.int32, (XEXT, 128), 0) - OFF
+    wfar_ref[...] = edge_table(128, 0, at)
+    wnear_ref[...] = edge_table(128, 4, at)
+    kinds = lax.broadcasted_iota(jnp.int32, (8, 384), 0)
+    high, low = split(edge_table(256, kinds, lax.broadcasted_iota(jnp.int32, (8, 384), 1)))
+    pick_ref[...] = jnp.concatenate([high.astype(F32), low.astype(F32)], axis=0).astype(BF16)
     vin.wait()
 
     part = 48
@@ -330,8 +345,9 @@
             for t in range(TILES):
                 x = None
                 for grid in grids:
-                    y = grid[pl.ds(first_row(t, z + 1) + 2 * r0, part, stride=2), :]
-                    x = y if x is None else x + y
+                    for at in spots(t, z + 1):
+                        y = grid[pl.ds(at + 2 * r0, part, stride=2), :]
+                        x = y if x is None else x + y
                 tiles.append(x)
             mcol = mxcol[r0 : r0 + part, :]
             wf, wn = wfar_ref[r0 : r0 + part, :], wnear_ref[r0 : r0 + part, :]
@@ -382,10 +398,12 @@
     lax.fori_loop(0, 16, plane, 0)
 
     corner = jnp.zeros((48, 128), F32)
+    kinds = jnp.minimum(lax.broadcasted_iota(jnp.int32, (384, 128), 1), 7)
+    tail = edge_table(256, kinds, lax.broadcasted_iota(jnp.int32, (384, 128), 0))
     for t in range(7):
         row = jnp.concatenate([rlp[h, pl.ds(t, 48, stride=8), :] for h in range(3)], axis=1)
         rl_ref[t] = row[:, 0:256]
-        ends = jnp.dot(row, tail_ref[...], preferred_element_type=F32, precision=lax.Precision.HIGHEST)
+        ends = jnp.dot(row, tail, preferred_element_type=F32, precision=lax.Precision.HIGHEST)
         corner = corner + (pltpu.roll(ends, 8 * t, 1) if t else ends)
         ud_ref[t] = udp[pl.ds(t, 48, stride=8), :]
     rl_ref[7] = jnp.zeros((48, 256), F32)
@@ -396,17 +414,7 @@
 
 
 def spread(inbox, mx, my, v):
-    ends = edge_weights(256, 384)
-    high, low = halves(ends)
-    pick = np.concatenate([high, low], axis=0)
-    tail = np.zeros((384, 128), np.float32)
-    tail[:, 0:8] = ends.T
-    weights = edge_weights(128, 144)
-    far = np.zeros((XEXT, 128), np.float32)
-    near = np.zeros((XEXT, 128), np.float32)
-    far[OFF : OFF + 128] = weights[0, 0:128, None]
-    near[OFF : OFF + 128] = weights[4, 0:128, None]
-    rows = TILES * PAIRS * 2 * XEXT
+    rows = TILES * 2 * PAIRS * SPAN
     total = inbox.shape[0] * SLOTS
     vm = pl.BlockSpec(memory_space=VMEM)
     return pl.pallas_call(
@@ -417,7 +425,7 @@
             jax.ShapeDtypeStruct((48, 128), F32),
             jax.ShapeDtypeStruct((8, 48, 128), F32),
         ),
-        in_specs=[vm] * 7 + [pl.BlockSpec(memory_space=pl.ANY)],
+        in_specs=[vm] * 3 + [pl.BlockSpec(memory_space=pl.ANY)],
         out_specs=(pl.BlockSpec(memory_space=pl.ANY), vm, vm, vm),
         scratch_shapes=[VMEM((rows, 128), F32)] * COPIES
         + [
@@ -427,6 +435,9 @@
             pltpu.SMEM((1, total), jnp.int32),
             VMEM((128, 128), F32),
             VMEM((XEXT, 128), F32),
+            VMEM((XEXT, 128), F32),
+            VMEM((XEXT, 128), F32),
+            VMEM((16, 384), BF16),
             VMEM((3, 3, XEXT, 128), F32),
             VMEM((3, 48 * 8, 128), F32),
             VMEM((48 * 8, 128), F32),
@@ -434,9 +445,10 @@
             pltpu.SemaphoreType.DMA((16,)),
             pltpu.SemaphoreType.DMA,
         ],
-        compiler_params=pltpu.CompilerParams(vmem_limit_bytes=60 << 20),
+        compiler_params=pltpu.CompilerParams(vmem_limit_bytes=45 << 20),
+        cost_estimate=cost(100 << 20),
         name="spread",
-    )(inbox, mx, my, pick, tail, far, near, v)
+    )(inbox, mx, my, v)
 
 
 def exchange_kernel(
@@ -562,7 +574,8 @@
             pltpu.SemaphoreType.DMA((8,)),
             pltpu.SemaphoreType.DMA((8,)),
         ],
-        compiler_params=pltpu.CompilerParams(collective_id=0, has_side_effects=True),
+        compiler_params=pltpu.CompilerParams(vmem_limit_bytes=8 << 20, collective_id=0, has_side_effects=True),
+        cost_estimate=cost(30 << 20),
         name="exchange",
     )(rl, cn, ud)
 
@@ -632,7 +645,8 @@
         in_specs=[block, xspec, yspec] + [whole(x) for x in (mx, my) + consts],
         out_specs=(block, block),
         scratch_shapes=[VMEM((128, 128), F32), VMEM((8, 256), F32)],
-        compiler_params=pltpu.CompilerParams(vmem_limit_bytes=62 << 20),
+        compiler_params=pltpu.CompilerParams(vmem_limit_bytes=24 << 20),
+        cost_estimate=cost(30 << 20),
         name="derive",
     )(e, xh, yh, mx, my, *consts)
 

time: 88.4 us -> 82.4 us (0.932)
  Pallas kernels: 87.4 us -> 79.1 us
  local copies, waits for them, and re-layouts: 0 us -> 2.32 us
    pallas_call x1, Pallas kernels: 42.3 us -> 36.2 us  [spread(): pl.pallas_call(spread_kernel, out_shape=(jax.ShapeDtypeStruct(v.shape, F3...]
    unnamed x0 -> x14, local copies, waits for them, and re-layouts: none -> 2.32 us
    pallas_call x1, Pallas kernels: 11 us -> 9.02 us  [derive(): pl.pallas_call(derive_kernel, grid=(n // each,), out_shape=(jax.ShapeDtyp...]
where the time goes in v3:
time: 82.4 us; the launch traced here: 82.1 us
  Pallas kernels  79.1 us (96%)
  local copies, waits for them, and re-layouts  2.32 us (3%)
    pallas_call x1, Pallas kernels, spread(): pl.pallas_call(spread_kernel, out_shape=(jax.ShapeDtypeStruct(v.shape, F3...  36.2 us
    pallas_call x1, Pallas kernels, shuffle(): pl.pallas_call(shuffle_kernel, out_shape=jax.ShapeDtypeStruct((nx, ny, 1,...  16.9 us
    pallas_call x1, Pallas kernels, exchange(): pl.pallas_call(exchange_kernel, out_shape=(jax.ShapeDtypeStruct((2, 8 * n...  12.5 us
    pallas_call x1, Pallas kernels, derive(): pl.pallas_call(derive_kernel, grid=(n // each,), out_shape=(jax.ShapeDtyp...  9.02 us
    pallas_call x1, Pallas kernels, pack(): pl.pallas_call(pack_kernel, out_shape=jax.ShapeDtypeStruct((8, counts.sha...  4.43 us
    unnamed x14, local copies, waits for them, and re-layouts  2.32 us

profile of v3, /device:TPU:1, one launch (start us, length us, event | category | flops | bytes accessed | tf_op | source)
XLA Modules:
  0.0 82.1 jit_solution(3616596475167806256)
XLA Ops:
  0.6 0.0 copy-start.4
  0.6 0.0 copy-start.1
  0.7 0.0 copy-start.2
  0.7 0.0 copy-start.3
  0.7 4.4 %pack.1.out_ref = f32[8,16,1,256]{3,2,1,0:T(1,128)} custom-call(s32[1,128]{1,0:T(1,128)} %counts_ref.1, f32[3,2048]{1,0:T(4,128)} %force_ref.1, f32[3,2048]{1,0:T(4,128)} %frac_ref.1, s32[16,128]{1,0:T(8,128)} %bitcast.15, s32[16,128]{1,0:T(8,128)} %bitcast.16, s32[16,128]{1,0:T(8,128)} %bitcast.17), custom_call_target="tpu_custom_call" | custom-call | bytes 12582912 | tf_op jit(solution)/shard_map/pack/pallas_call | solution.py:110
  5.1 16.9 %shuffle.1 = f32[16,8,1,256]{3,2,1,0:T(1,128)} custom-call(f32[8,16,1,256]{3,2,1,0:T(1,128)} %pack.1.out_ref), custom_call_target="tpu_custom_call" | custom-call | bytes 37748736 | tf_op jit(solution)/shard_map/shuffle/pallas_call | solution.py:164
  22.1 0.0 copy-start
  22.1 0.9 %copy-done = f32[16,8,1,256]{3,2,1,0:T(1,128)S(1)} copy-done((f32[16,8,1,256]{3,2,1,0:T(1,128)S(1)}, f32[16,8,1,256]{3,2,1,0:T(1,128)}, u32[]{:S(2)}) %copy-start) | copy-done | bytes 131096
  23.0 0.0 copy-start.5
  23.0 0.7 copy-done.5
  23.7 0.0 copy-start.6
  23.7 0.7 copy-done.6
  24.4 36.2 %spread.1 = (f32[3,16,128,256]{3,2,1,0:T(8,128)S(1)}, f32[8,48,256]{2,1,0:T(8,128)S(1)}, f32[48,128]{1,0:T(8,128)S(1)}, f32[8,48,128]{2,1,0:T(8,128)S(1)}) custom-call(f32[128,1,256]{2,1,0:T(1,128)S(1)} %bitcast.10, f32[16,128]{1,0:T(8,128)S(1)} %bitcast.11, f32[16,128]{1,0:T(8,128)S(1)} %bitcast.13, f32[3,16,128,256]{3,2,1,0:T(8,128)} %v_hbm.1), custom_call_target="tpu_custom_call" | custom-call | bytes 104857600 | tf_op jit(solution)/shard_map/spread/pallas_call | solution.py:420
  60.6 12.5 %exchange.1 = (f32[2,384,128]{2,1,0:T(8,128)S(1)}, f32[384,128]{1,0:T(8,128)S(1)}) custom-call(f32[8,48,256]{2,1,0:T(8,128)S(1)} %get-tuple-element.11.rl_hbm, f32[48,128]{1,0:T(8,128)S(1)} %get-tuple-element.12.cn_hbm, f32[8,48,128]{2,1,0:T(8,128)S(1)} %get-tuple-element.13.ud_hbm), custom_call_target="tpu_custom_call" | custom-call | bytes 31457280 | tf_op jit(solution)/shard_map/exchange/pallas_call | solution.py:554
  73.0 0.0 copy-done.4
  73.1 0.0 copy-done.1
  73.1 0.0 copy-done.2
  73.1 0.0 copy-done.3
  73.1 9.0 %derive.1 = (f32[48,128,256]{2,1,0:T(8,128)}, f32[48,128,256]{2,1,0:T(8,128)}) custom-call(f32[48,128,256]{2,1,0:T(8,128)S(1)} %bitcast.9, f32[2,384,128]{2,1,0:T(8,128)S(1)} %get-tuple-element.14.xh_ref, f32[384,128]{1,0:T(8,128)S(1)} %get-tuple-element.15.yh_ref, f32[16,128]{1,0:T(8,128)S(1)} %bitcast.12, f32[16,128]{1,0:T(8,128)S(1)} %bitcast.14, ...), custom_call_target="tpu_custom_call" | custom-call | bytes 31457280 | tf_op jit(solution)/shard_map/derive/pallas_call | solution.py:641
Async XLA Ops:
  0.6 72.4 %copy-start.4 = (bf16[32,512]{1,0:T(8,128)(2,1)S(1)}, bf16[32,512]{1,0:T(8,128)(2,1)}, u32[]{:S(2)}) copy-start(bf16[32,512]{1,0:T(8,128)(2,1)} %constant.11.clone.rim_ref) | copy-start | bytes 98308
  0.6 72.4 %copy-start.1 = (bf16[256,256]{1,0:T(8,128)(2,1)S(1)}, bf16[256,256]{1,0:T(8,128)(2,1)}, u32[]{:S(2)}) copy-start(bf16[256,256]{1,0:T(8,128)(2,1)} %constant.10.clone.kl_ref) | copy-start | bytes 393220
  0.7 72.4 %copy-start.2 = (bf16[256,256]{1,0:T(8,128)(2,1)S(1)}, bf16[256,256]{1,0:T(8,128)(2,1)}, u32[]{:S(2)}) copy-start(bf16[256,256]{1,0:T(8,128)(2,1)} %constant.9.clone.ky_ref) | copy-start | bytes 393220
  0.7 72.4 %copy-start.3 = (bf16[256,144]{1,0:T(8,128)(2,1)S(1)}, bf16[256,144]{1,0:T(8,128)(2,1)}, u32[]{:S(2)}) copy-start(bf16[256,144]{1,0:T(8,128)(2,1)} %constant.8.clone.kx_ref) | copy-start | bytes 221188
  22.1 0.9 %copy-start = (f32[16,8,1,256]{3,2,1,0:T(1,128)S(1)}, f32[16,8,1,256]{3,2,1,0:T(1,128)}, u32[]{:S(2)}) copy-start(f32[16,8,1,256]{3,2,1,0:T(1,128)} %shuffle.1) | copy-start | bytes 393220
  23.0 0.7 copy-start.5
  23.7 0.7 copy-start.6

commit v4 on v3

--- a/solution.py
+++ b/solution.py
@@ -17,7 +17,9 @@
 XEXT = 144
 PAIRS = 9
 SPAN = 2 * XEXT
-EACH = 8
+EACH = 12
+UNROLL = 4
+TOGETHER = 4
 TILES = 7
 COPIES = 2
 ROOT = (math.sqrt(5.0) - 3.0) / 2.0
@@ -80,6 +82,7 @@
     lane = lax.broadcasted_iota(jnp.int32, (8, 128), 1)
     sub = lax.broadcasted_iota(jnp.int32, (8, 128), 0)
     part = sub & 3
+    unused = jnp.where((sub == 6) & (lane < SLOTS), lane * (4 << 12), 0).astype(F32)
 
     def one(d, start):
         count = counts_ref[0, d]
@@ -89,7 +92,7 @@
         a = pltpu.roll(wide[:, pl.ds(first, 128)], back, 1)
         b = pltpu.roll(wide[:, pl.ds(first + 128, 128)], back, 1)
         w = jnp.where(lane + shift < 128, a, b)
-        w = jnp.where(lane < count, w, 0.0)
+        w = jnp.where(lane < count, w, unused)
         m = w
         for j in range(1, 4):
             m = jnp.where(part == j, pltpu.roll(w, SLOTS * j, 1), m)
@@ -97,12 +100,13 @@
         low = jnp.sum(jnp.where(sub < 4, 0.0, m), axis=0, keepdims=True)
         return start + count, jnp.concatenate([top, low], axis=1)
 
-    def eight(g, start):
-        for k in range(8):
-            start, out_ref[k, g] = one(g * 8 + k, start)
+    def several(g, start):
+        for j in range(UNROLL):
+            for k in range(8):
+                start, out_ref[k, g * UNROLL + j] = one((g * UNROLL + j) * 8 + k, start)
         return start
 
-    lax.fori_loop(0, out_ref.shape[1], eight, jnp.int32(0))
+    lax.fori_loop(0, out_ref.shape[1] // UNROLL, several, jnp.int32(0))
 
 
 def pack(counts, *fields):
@@ -196,7 +200,7 @@
     inside = (spots >= 0) & (spots < n)
     steps = jnp.where(kinds == 0, n - 1 - spots, spots)
     sums = jnp.where(inside & ((kinds == 0) | (kinds == 4)), powers(jnp.where(inside, steps, 0)), 0.0)
-    only = jnp.where(kinds < 4, n - 2 + kinds, jnp.where(kinds == 5, 0, n + 2))
+    only = jnp.where(kinds < 4, n - 2 + kinds, jnp.where(kinds == 5, 0, n + 127))
     single = (kinds != 0) & (kinds != 4) & (kinds < 7) & (spots == only)
     return jnp.where(single, 1.0, sums)
 
@@ -207,7 +211,7 @@
     *scratch,
 ):
     grids = scratch[:COPIES]
-    vbuf, m8, base_v, base_s, fcy, mxcol, wfar_ref, wnear_ref, pick_ref, ext, rlp, udp, v_sem, e_sems, s_sem = scratch[COPIES:]
+    vbuf, m8, base_v, base_s, mxcol, wfar_ref, wnear_ref, pick_ref, ext, rlp, udp, v_sem, e_sems, s_sem = scratch[COPIES:]
     gx, gy = lax.axis_index("gx"), lax.axis_index("gy")
     chunks = inbox_ref.shape[0] * SLOTS // 128
     vin = pltpu.make_async_copy(v_hbm, vbuf, v_sem)
@@ -259,7 +263,7 @@
     comp = jnp.where(sub2 >= 2 * GROUP, 2, jnp.where(sub2 >= GROUP, 1, 0))
     rel = jnp.where(sub2 >= 3 * GROUP, -100, sub2 - GROUP * comp)
 
-    def chunk(c, carry):
+    def tables(c):
         m = m8[:, pl.ds(pl.multiple_of(c * 128, 128), 128)]
         ws = stencil_weights(m)
         code = m[6:7].astype(jnp.int32)
@@ -271,26 +275,27 @@
         w = jnp.where(d == 2, ws[2][4:5], w)
         w = jnp.where(d == 3, ws[3][4:5], w)
         f = jnp.where(comp == 0, m[0:1], jnp.where(comp == 1, m[1:2], m[2:3]))
-        fcy[...] = jnp.transpose(w * f)
-        wx = [w[3:4] for w in ws]
-        wz = [w[5:6] for w in ws]
-        sides = ((wz[0], wz[1]), (wz[2], wz[3]))
-        wx8 = jnp.concatenate([wx[i // 2] for i in range(8)], axis=0)
+        wx8 = jnp.concatenate([ws[i // 2][3:4] for i in range(8)], axis=0)
+        sides = ((ws[0][5:6], ws[1][5:6]), (ws[2][5:6], ws[3][5:6]))
         tall = [wx8 * jnp.concatenate(list(side) * 4, axis=0) for side in sides]
-        fr = fcy[...]
-        bs = [base_s[0, c * 128 + k] for k in range(128)]
-        for k0 in range(0, 128, COPIES):
-            group = []
-            for k in range(k0, k0 + COPIES):
-                grid = grids[k % COPIES]
-                for q in range(2):
-                    at = bs[k] + q * SPAN
-                    group.append((grid, at, grid[pl.ds(at, 8), :] + tall[q][:, k : k + 1] * fr[k : k + 1, :]))
-            for grid, at, value in group:
-                grid[pl.ds(at, 8), :] = value
+        return jnp.transpose(w * f), tall
+
+    def chunk(i, carry):
+        built = [tables(i * TOGETHER + j) for j in range(TOGETHER)]
+        for j, (fr, tall) in enumerate(built):
+            bs = [base_s[0, (i * TOGETHER + j) * 128 + k] for k in range(128)]
+            for k0 in range(0, 128, COPIES):
+                group = []
+                for k in range(k0, k0 + COPIES):
+                    grid = grids[k % COPIES]
+                    for q in range(2):
+                        at = bs[k] + q * SPAN
+                        group.append((grid, at, grid[pl.ds(at, 8), :] + tall[q][:, k : k + 1] * fr[k : k + 1, :]))
+                for grid, at, value in group:
+                    grid[pl.ds(at, 8), :] = value
         return carry
 
-    lax.fori_loop(0, chunks, chunk, 0)
+    lax.fori_loop(0, chunks // TOGETHER, chunk, 0)
 
     def spots(t, e, odds=(0, 1)):
         return [(2 * t + odd) * PAIRS * SPAN + ((e - odd) >> 1) * SPAN + ((e - odd) & 1) for odd in odds]
@@ -310,9 +315,9 @@
     mxcol[OFF : OFF + 128, :] = row_as_column(mx_ref[pl.ds(gx, 1), :])
     mxcol[OFF + 128 : XEXT, :] = row_as_column(mx_ref[pl.ds(lax.rem(gx + 1, nx), 1), :])[0 : XEXT - OFF - 128]
     after = my_ref[pl.ds(lax.rem(2 * gy + 2, ny), 1), :]
-    before = pltpu.roll(jnp.broadcast_to(my_ref[pl.ds(lax.rem(2 * gy + ny - 1, ny), 1), :], (8, 128)), 3, 1)[0:1]
+    before = my_ref[pl.ds(lax.rem(2 * gy + ny - 1, ny), 1), :]
     lane1 = lax.broadcasted_iota(jnp.int32, (1, 128), 1)
-    rim = jnp.where(lane1 < 2, after, jnp.where(lane1 == 2, before, 0.0))
+    rim = jnp.where(lane1 < 2, after, jnp.where(lane1 == 127, before, 0.0))
     mys = [HALF * my_ref[pl.ds(2 * gy, 1), :], HALF * my_ref[pl.ds(2 * gy + 1, 1), :], HALF * rim]
     at = lax.broadcasted_iota(jnp.int32, (XEXT, 128), 0) - OFF
     wfar_ref[...] = edge_table(128, 0, at)
@@ -325,16 +330,12 @@
     part = 48
     lanes = lax.broadcasted_iota(jnp.int32, (part, 128), 1)
 
-    def moves(c, h):
-        out = []
-        if h == 2:
-            out.append((6, (-(GROUP * c + 256 - (6 * BASES - 1))) % 128, 0, 2))
-            out.append((0, (2 - GROUP * c) % 128, 2, 3))
-            return out
+    def moves(h):
+        out = [(6, 0, 2), (0, 127, 128)] if h == 2 else []
         for t in range(TILES):
             low, high = BASES * t - 1 - 128 * h, BASES * t - 1 + GROUP - 128 * h
-            if high > 0 and low < 128:
-                out.append((t, (low - GROUP * c) % 128, max(low, 0), min(high, 128)))
+            if h < 2 and high > 0 and low < 128:
+                out.append((t, max(low, 0), min(high, 128)))
         return out
 
     def plane(z, carry):
@@ -354,10 +355,11 @@
             r1 = r0 + part
             i0, i1 = max(r0, OFF), min(r1, OFF + 128)
             for c in range(3):
+                turned = [pltpu.roll(tiles[t], (BASES * t - 1 - GROUP * c) % 128, 1) for t in range(TILES)]
                 for h in range(3):
                     e = None
-                    for t, turn, low, high in moves(c, h):
-                        x = pltpu.roll(tiles[t], turn, 1) if turn else tiles[t]
+                    for t, low, high in moves(h):
+                        x = turned[t]
                         if low > 0 or high < 128:
                             x = jnp.where((lanes >= low) & (lanes < high), x, 0.0)
                         e = x if e is None else e + x
@@ -433,7 +435,6 @@
             VMEM((8, total), F32),
             VMEM((1, total), jnp.int32),
             pltpu.SMEM((1, total), jnp.int32),
-            VMEM((128, 128), F32),
             VMEM((XEXT, 128), F32),
             VMEM((XEXT, 128), F32),
             VMEM((XEXT, 128), F32),
@@ -645,7 +646,7 @@
         in_specs=[block, xspec, yspec] + [whole(x) for x in (mx, my) + consts],
         out_specs=(block, block),
         scratch_shapes=[VMEM((128, 128), F32), VMEM((8, 256), F32)],
-        compiler_params=pltpu.CompilerParams(vmem_limit_bytes=24 << 20),
+        compiler_params=pltpu.CompilerParams(vmem_limit_bytes=30 << 20),
         cost_estimate=cost(30 << 20),
         name="derive",
     )(e, xh, yh, mx, my, *consts)

time: 82.4 us -> 76.4 us (0.927)
  Pallas kernels: 79.1 us -> 73.1 us
    pallas_call x1, Pallas kernels: 36.2 us -> 32.2 us  [spread(): pl.pallas_call(spread_kernel, out_shape=(jax.ShapeDtypeStruct(v.shape, F3...]
    pallas_call x1, Pallas kernels: 4.43 us -> 3.02 us  [pack(): pl.pallas_call(pack_kernel, out_shape=jax.ShapeDtypeStruct((8, counts.sha...]
where the time goes in v4:
time: 76.4 us; the launch traced here: 76.2 us
  Pallas kernels  73.1 us (96%)
  local copies, waits for them, and re-layouts  2.32 us (3%)
    pallas_call x1, Pallas kernels, spread(): pl.pallas_call(spread_kernel, out_shape=(jax.ShapeDtypeStruct(v.shape, F3...  32.2 us
    pallas_call x1, Pallas kernels, shuffle(): pl.pallas_call(shuffle_kernel, out_shape=jax.ShapeDtypeStruct((nx, ny, 1,...  16.9 us
    pallas_call x1, Pallas kernels, exchange(): pl.pallas_call(exchange_kernel, out_shape=(jax.ShapeDtypeStruct((2, 8 * n...  12.2 us
    pallas_call x1, Pallas kernels, derive(): pl.pallas_call(derive_kernel, grid=(n // each,), out_shape=(jax.ShapeDtyp...  8.76 us
    pallas_call x1, Pallas kernels, pack(): pl.pallas_call(pack_kernel, out_shape=jax.ShapeDtypeStruct((8, counts.sha...  3.02 us
    unnamed x14, local copies, waits for them, and re-layouts  2.32 us

profile of v4, /device:TPU:1, one launch (start us, length us, event | category | flops | bytes accessed | tf_op | source)
XLA Modules:
  0.0 76.2 jit_solution(2792193318790364986)
XLA Ops:
  0.6 0.0 copy-start.4
  0.6 0.0 copy-start.1
  0.7 0.0 copy-start.2
  0.7 0.0 copy-start.3
  0.7 3.0 %pack.1.out_ref = f32[8,16,1,256]{3,2,1,0:T(1,128)} custom-call(s32[1,128]{1,0:T(1,128)} %counts_ref.1, f32[3,2048]{1,0:T(4,128)} %force_ref.1, f32[3,2048]{1,0:T(4,128)} %frac_ref.1, s32[16,128]{1,0:T(8,128)} %bitcast.15, s32[16,128]{1,0:T(8,128)} %bitcast.16, s32[16,128]{1,0:T(8,128)} %bitcast.17), custom_call_target="tpu_custom_call" | custom-call | bytes 12582912 | tf_op jit(solution)/shard_map/pack/pallas_call | solution.py:114
  3.7 16.9 %shuffle.1 = f32[16,8,1,256]{3,2,1,0:T(1,128)} custom-call(f32[8,16,1,256]{3,2,1,0:T(1,128)} %pack.1.out_ref), custom_call_target="tpu_custom_call" | custom-call | bytes 37748736 | tf_op jit(solution)/shard_map/shuffle/pallas_call | solution.py:168
  20.7 0.0 copy-start
  20.7 0.9 %copy-done = f32[16,8,1,256]{3,2,1,0:T(1,128)S(1)} copy-done((f32[16,8,1,256]{3,2,1,0:T(1,128)S(1)}, f32[16,8,1,256]{3,2,1,0:T(1,128)}, u32[]{:S(2)}) %copy-start) | copy-done | bytes 131096
  21.6 0.0 copy-start.5
  21.6 0.7 copy-done.5
  22.3 0.0 copy-start.6
  22.3 0.7 copy-done.6
  23.0 32.2 %spread.1 = (f32[3,16,128,256]{3,2,1,0:T(8,128)S(1)}, f32[8,48,256]{2,1,0:T(8,128)S(1)}, f32[48,128]{1,0:T(8,128)S(1)}, f32[8,48,128]{2,1,0:T(8,128)S(1)}) custom-call(f32[128,1,256]{2,1,0:T(1,128)S(1)} %bitcast.10, f32[16,128]{1,0:T(8,128)S(1)} %bitcast.11, f32[16,128]{1,0:T(8,128)S(1)} %bitcast.13, f32[3,16,128,256]{3,2,1,0:T(8,128)} %v_hbm.1), custom_call_target="tpu_custom_call" | custom-call | bytes 104857600 | tf_op jit(solution)/shard_map/spread/pallas_call | solution.py:422
  55.1 12.2 %exchange.1 = (f32[2,384,128]{2,1,0:T(8,128)S(1)}, f32[384,128]{1,0:T(8,128)S(1)}) custom-call(f32[8,48,256]{2,1,0:T(8,128)S(1)} %get-tuple-element.11.rl_hbm, f32[48,128]{1,0:T(8,128)S(1)} %get-tuple-element.12.cn_hbm, f32[8,48,128]{2,1,0:T(8,128)S(1)} %get-tuple-element.13.ud_hbm), custom_call_target="tpu_custom_call" | custom-call | bytes 31457280 | tf_op jit(solution)/shard_map/exchange/pallas_call | solution.py:555
  67.4 0.0 copy-done.4
  67.4 0.0 copy-done.1
  67.4 0.0 copy-done.2
  67.4 0.0 copy-done.3
  67.4 8.8 %derive.1 = (f32[48,128,256]{2,1,0:T(8,128)}, f32[48,128,256]{2,1,0:T(8,128)}) custom-call(f32[48,128,256]{2,1,0:T(8,128)S(1)} %bitcast.9, f32[2,384,128]{2,1,0:T(8,128)S(1)} %get-tuple-element.14.xh_ref, f32[384,128]{1,0:T(8,128)S(1)} %get-tuple-element.15.yh_ref, f32[16,128]{1,0:T(8,128)S(1)} %bitcast.12, f32[16,128]{1,0:T(8,128)S(1)} %bitcast.14, ...), custom_call_target="tpu_custom_call" | custom-call | bytes 31457280 | tf_op jit(solution)/shard_map/derive/pallas_call | solution.py:642
Async XLA Ops:
  0.6 66.8 %copy-start.4 = (bf16[32,512]{1,0:T(8,128)(2,1)S(1)}, bf16[32,512]{1,0:T(8,128)(2,1)}, u32[]{:S(2)}) copy-start(bf16[32,512]{1,0:T(8,128)(2,1)} %constant.11.clone.rim_ref) | copy-start | bytes 98308
  0.6 66.8 %copy-start.1 = (bf16[256,256]{1,0:T(8,128)(2,1)S(1)}, bf16[256,256]{1,0:T(8,128)(2,1)}, u32[]{:S(2)}) copy-start(bf16[256,256]{1,0:T(8,128)(2,1)} %constant.10.clone.kl_ref) | copy-start | bytes 393220
  0.7 66.8 %copy-start.2 = (bf16[256,256]{1,0:T(8,128)(2,1)S(1)}, bf16[256,256]{1,0:T(8,128)(2,1)}, u32[]{:S(2)}) copy-start(bf16[256,256]{1,0:T(8,128)(2,1)} %constant.9.clone.ky_ref) | copy-start | bytes 393220
  0.7 66.8 %copy-start.3 = (bf16[256,144]{1,0:T(8,128)(2,1)S(1)}, bf16[256,144]{1,0:T(8,128)(2,1)}, u32[]{:S(2)}) copy-start(bf16[256,144]{1,0:T(8,128)(2,1)} %constant.8.clone.kx_ref) | copy-start | bytes 221188
  20.7 0.9 %copy-start = (f32[16,8,1,256]{3,2,1,0:T(1,128)S(1)}, f32[16,8,1,256]{3,2,1,0:T(1,128)}, u32[]{:S(2)}) copy-start(f32[16,8,1,256]{3,2,1,0:T(1,128)} %shuffle.1) | copy-start | bytes 393220
  21.6 0.7 copy-start.5
  22.3 0.7 copy-start.6

commit v5 on v4

--- a/solution.py
+++ b/solution.py
@@ -18,6 +18,7 @@
 PAIRS = 9
 SPAN = 2 * XEXT
 EACH = 12
+METRIC = 8
 UNROLL = 4
 TOGETHER = 4
 TILES = 7
@@ -122,11 +123,16 @@
     )(counts, *fields)
 
 
-def shuffle_kernel(out_ref, in_ref, mid, own_sems, send_y, recv_y, send_x, recv_x):
+def shuffle_kernel(out_ref, mx_ref, my_ref, in_ref, mid, own_sems, send_y, recv_y, send_x, recv_x):
     gx, gy = lax.axis_index("gx"), lax.axis_index("gy")
     nx, ny = lax.axis_size("gx"), lax.axis_size("gy")
     own = pltpu.make_async_copy(out_ref.at[gy], mid.at[gy], own_sems.at[0])
     own.start()
+    metrics = [
+        pltpu.make_async_copy(src, in_ref.at[nx + i], own_sems.at[2 + i]) for i, src in enumerate((mx_ref, my_ref))
+    ]
+    for copy in metrics:
+        copy.start()
     barrier = pltpu.get_barrier_semaphore()
     for k in range(1, ny):
         pl.semaphore_signal(barrier, inc=1, device_id=(gx, lax.rem(gy + k, ny)), device_id_type=MESH)
@@ -157,24 +163,24 @@
         copy.start()
         copies.append(copy)
     own.wait()
-    for copy in copies:
+    for copy in copies + metrics:
         copy.wait()
 
 
-def shuffle(outbox):
+def shuffle(outbox, mx, my):
     ny, nx = outbox.shape[0:2]
     anywhere = pl.BlockSpec(memory_space=pl.ANY)
     dma = pltpu.SemaphoreType.DMA
     return pl.pallas_call(
         shuffle_kernel,
-        out_shape=jax.ShapeDtypeStruct((nx, ny, 1, 256), F32),
-        in_specs=[anywhere],
+        out_shape=jax.ShapeDtypeStruct((nx + 2, ny, 1, 256), F32),
+        in_specs=[anywhere] * 3,
         out_specs=anywhere,
-        scratch_shapes=[VMEM((ny, nx, 1, 256), F32), dma((2,)), dma((ny,)), dma((ny,)), dma((nx,)), dma((nx,))],
+        scratch_shapes=[VMEM((ny, nx, 1, 256), F32), dma((4,)), dma((ny,)), dma((ny,)), dma((nx,)), dma((nx,))],
         compiler_params=pltpu.CompilerParams(collective_id=1, has_side_effects=True),
         cost_estimate=cost(36 << 20),
         name="shuffle",
-    )(outbox)
+    )(outbox, mx, my)
 
 
 def row_as_column(row):
@@ -206,14 +212,15 @@
 
 
 def spread_kernel(
-    inbox_ref, mx_ref, my_ref, v_hbm,
+    inbox_ref, v_hbm,
     e_hbm, rl_ref, cn_ref, ud_ref,
     *scratch,
 ):
     grids = scratch[:COPIES]
     vbuf, m8, base_v, base_s, mxcol, wfar_ref, wnear_ref, pick_ref, ext, rlp, udp, v_sem, e_sems, s_sem = scratch[COPIES:]
     gx, gy = lax.axis_index("gx"), lax.axis_index("gy")
-    chunks = inbox_ref.shape[0] * SLOTS // 128
+    messages = inbox_ref.shape[0] - 2 * METRIC
+    chunks = messages * SLOTS // 128
     vin = pltpu.make_async_copy(v_hbm, vbuf, v_sem)
     vin.start()
     lane = lax.broadcasted_iota(jnp.int32, (8, 128), 1)
@@ -310,15 +317,23 @@
             here = pl.ds(spots(t, dst)[0], XEXT, stride=2)
             grids[0][here, :] = grids[0][here, :] + moved
 
-    nx, ny = mx_ref.shape[0], my_ref.shape[0]
-    mxcol[0:OFF, :] = row_as_column(mx_ref[pl.ds(lax.rem(gx + nx - 1, nx), 1), :])[128 - OFF : 128]
-    mxcol[OFF : OFF + 128, :] = row_as_column(mx_ref[pl.ds(gx, 1), :])
-    mxcol[OFF + 128 : XEXT, :] = row_as_column(mx_ref[pl.ds(lax.rem(gx + 1, nx), 1), :])[0 : XEXT - OFF - 128]
-    after = my_ref[pl.ds(lax.rem(2 * gy + 2, ny), 1), :]
-    before = my_ref[pl.ds(lax.rem(2 * gy + ny - 1, ny), 1), :]
+    def along_x(i):
+        i = lax.rem(i, 2 * METRIC)
+        pair = inbox_ref[messages + (i >> 1)]
+        return row_as_column(jnp.where((i & 1) == 1, pair[:, 128:256], pair[:, 0:128]))
+
+    def along_y(i):
+        return inbox_ref[messages + METRIC + lax.rem(i, METRIC)]
+
+    mxcol[0:OFF, :] = along_x(gx + 2 * METRIC - 1)[128 - OFF : 128]
+    mxcol[OFF : OFF + 128, :] = along_x(gx)
+    mxcol[OFF + 128 : XEXT, :] = along_x(gx + 1)[0 : XEXT - OFF - 128]
+    after = along_y(gy + 1)[:, 0:128]
+    before = along_y(gy + METRIC - 1)[:, 128:256]
+    here = along_y(gy)
     lane1 = lax.broadcasted_iota(jnp.int32, (1, 128), 1)
     rim = jnp.where(lane1 < 2, after, jnp.where(lane1 == 127, before, 0.0))
-    mys = [HALF * my_ref[pl.ds(2 * gy, 1), :], HALF * my_ref[pl.ds(2 * gy + 1, 1), :], HALF * rim]
+    mys = [HALF * here[:, 0:128], HALF * here[:, 128:256], HALF * rim]
     at = lax.broadcasted_iota(jnp.int32, (XEXT, 128), 0) - OFF
     wfar_ref[...] = edge_table(128, 0, at)
     wnear_ref[...] = edge_table(128, 4, at)
@@ -402,12 +417,17 @@
     corner = jnp.zeros((48, 128), F32)
     kinds = jnp.minimum(lax.broadcasted_iota(jnp.int32, (384, 128), 1), 7)
     tail = edge_table(256, kinds, lax.broadcasted_iota(jnp.int32, (384, 128), 0))
+    lines = []
     for t in range(7):
         row = jnp.concatenate([rlp[h, pl.ds(t, 48, stride=8), :] for h in range(3)], axis=1)
         rl_ref[t] = row[:, 0:256]
-        ends = jnp.dot(row, tail, preferred_element_type=F32, precision=lax.Precision.HIGHEST)
-        corner = corner + (pltpu.roll(ends, 8 * t, 1) if t else ends)
         ud_ref[t] = udp[pl.ds(t, 48, stride=8), :]
+        lines.append(row)
+    lines = jnp.concatenate(lines, axis=0)
+    ends = jnp.dot(lines, tail, preferred_element_type=F32, precision=lax.Precision.HIGHEST)
+    for t in range(7):
+        end = ends[t * 48 : (t + 1) * 48]
+        corner = corner + (pltpu.roll(end, 8 * t, 1) if t else end)
     rl_ref[7] = jnp.zeros((48, 256), F32)
     ud_ref[7] = jnp.zeros((48, 128), F32)
     cn_ref[...] = corner
@@ -415,9 +435,9 @@
         pltpu.make_async_copy(vbuf.at[:, z], e_hbm.at[:, z], e_sems.at[z]).wait()
 
 
-def spread(inbox, mx, my, v):
-    rows = TILES * 2 * PAIRS * SPAN
-    total = inbox.shape[0] * SLOTS
+def spread(inbox, v):
+    rows = TILES * 2 * PAIRS * SPAN + 8
+    total = (inbox.shape[0] - 2 * METRIC) * SLOTS
     vm = pl.BlockSpec(memory_space=VMEM)
     return pl.pallas_call(
         spread_kernel,
@@ -427,7 +447,7 @@
             jax.ShapeDtypeStruct((48, 128), F32),
             jax.ShapeDtypeStruct((8, 48, 128), F32),
         ),
-        in_specs=[vm] * 3 + [pl.BlockSpec(memory_space=pl.ANY)],
+        in_specs=[vm] + [pl.BlockSpec(memory_space=pl.ANY)],
         out_specs=(pl.BlockSpec(memory_space=pl.ANY), vm, vm, vm),
         scratch_shapes=[VMEM((rows, 128), F32)] * COPIES
         + [
@@ -449,7 +469,7 @@
         compiler_params=pltpu.CompilerParams(vmem_limit_bytes=45 << 20),
         cost_estimate=cost(100 << 20),
         name="spread",
-    )(inbox, mx, my, v)
+    )(inbox, v)
 
 
 def exchange_kernel(
@@ -659,9 +679,10 @@
     fold = lambda x: x.reshape(-1, 128)
     cells = [fold(x) for x in (marker_cell_x, marker_cell_y, marker_cell_z)]
     outbox = pack(send_counts, marker_force, marker_frac, *cells)
-    inbox = shuffle(outbox).reshape(-1, 1, 256)
+    slab = lambda x: x.reshape(METRIC, 1, 256)
+    inbox = shuffle(outbox, slab(metric_x), slab(metric_y)).reshape(-1, 1, 256)
     mx, my = fold(metric_x), fold(metric_y)
-    e, rl, cn, ud = spread(inbox, mx, my, velocity)
+    e, rl, cn, ud = spread(inbox, velocity)
     xh, yh = exchange(rl, cn, ud)
     dx, dy = derive(e.reshape(comps * planes, rows, cols), xh, yh, mx, my)
     return dx.reshape(velocity.shape), dy.reshape(velocity.shape)

time: 76.4 us -> 75.4 us (0.987)
  local copies, waits for them, and re-layouts: 2.32 us -> 0.94 us
    unnamed x14, local copies, waits for them, and re-layouts: 2.32 us -> 0.94 us
where the time goes in v5:
time: 75.4 us; the launch traced here: 75.2 us
  Pallas kernels  73.5 us (97%)
  local copies, waits for them, and re-layouts  0.94 us (1%)
  between operations  0.76 us (1%)
    pallas_call x1, Pallas kernels, spread(): pl.pallas_call(spread_kernel, out_shape=(jax.ShapeDtypeStruct(v.shape, F3...  32.5 us
    pallas_call x1, Pallas kernels, shuffle(): pl.pallas_call(shuffle_kernel, out_shape=jax.ShapeDtypeStruct((nx + 2, ny...  17 us
    pallas_call x1, Pallas kernels, exchange(): pl.pallas_call(exchange_kernel, out_shape=(jax.ShapeDtypeStruct((2, 8 * n...  12.2 us
    pallas_call x1, Pallas kernels, derive(): pl.pallas_call(derive_kernel, grid=(n // each,), out_shape=(jax.ShapeDtyp...  8.75 us
    pallas_call x1, Pallas kernels, pack(): pl.pallas_call(pack_kernel, out_shape=jax.ShapeDtypeStruct((8, counts.sha...  3.05 us

profile of v5, /device:TPU:1, one launch (start us, length us, event | category | flops | bytes accessed | tf_op | source)
XLA Modules:
  0.0 75.2 jit_solution(5323150968498772599)
XLA Ops:
  0.6 0.0 copy-start.4
  0.6 0.0 copy-start.1
  0.7 0.0 copy-start.2
  0.7 0.0 copy-start.3
  0.7 0.0 copy-start.6
  0.7 0.0 copy-start.5
  0.7 3.1 %pack.1.out_ref = f32[8,16,1,256]{3,2,1,0:T(1,128)} custom-call(s32[1,128]{1,0:T(1,128)} %counts_ref.1, f32[3,2048]{1,0:T(4,128)} %force_ref.1, f32[3,2048]{1,0:T(4,128)} %frac_ref.1, s32[16,128]{1,0:T(8,128)} %bitcast.17, s32[16,128]{1,0:T(8,128)} %bitcast.18, s32[16,128]{1,0:T(8,128)} %bitcast.19), custom_call_target="tpu_custom_call" | custom-call | bytes 12582912 | tf_op jit(solution)/shard_map/pack/pallas_call | solution.py:115
  3.8 17.0 %shuffle.1 = f32[18,8,1,256]{3,2,1,0:T(1,128)} custom-call(f32[8,16,1,256]{3,2,1,0:T(1,128)} %pack.1.out_ref, f32[8,1,256]{2,1,0:T(1,128)} %bitcast.13, f32[8,1,256]{2,1,0:T(1,128)} %bitcast.15), custom_call_target="tpu_custom_call" | custom-call | bytes 37748736 | tf_op jit(solution)/shard_map/shuffle/pallas_call | solution.py:174
  20.8 0.0 copy-start
  20.8 0.9 %copy-done = f32[18,8,1,256]{3,2,1,0:T(1,128)S(1)} copy-done((f32[18,8,1,256]{3,2,1,0:T(1,128)S(1)}, f32[18,8,1,256]{3,2,1,0:T(1,128)}, u32[]{:S(2)}) %copy-start) | copy-done | bytes 147480
  21.7 32.5 %spread.1 = (f32[3,16,128,256]{3,2,1,0:T(8,128)S(1)}, f32[8,48,256]{2,1,0:T(8,128)S(1)}, f32[48,128]{1,0:T(8,128)S(1)}, f32[8,48,128]{2,1,0:T(8,128)S(1)}) custom-call(f32[144,1,256]{2,1,0:T(1,128)S(1)} %bitcast.12, f32[3,16,128,256]{3,2,1,0:T(8,128)} %v_hbm.1), custom_call_target="tpu_custom_call" | custom-call | bytes 104857600 | tf_op jit(solution)/shard_map/spread/pallas_call | solution.py:442
  54.2 12.2 %exchange.1 = (f32[2,384,128]{2,1,0:T(8,128)S(1)}, f32[384,128]{1,0:T(8,128)S(1)}) custom-call(f32[8,48,256]{2,1,0:T(8,128)S(1)} %get-tuple-element.11.rl_hbm, f32[48,128]{1,0:T(8,128)S(1)} %get-tuple-element.12.cn_hbm, f32[8,48,128]{2,1,0:T(8,128)S(1)} %get-tuple-element.13.ud_hbm), custom_call_target="tpu_custom_call" | custom-call | bytes 31457280 | tf_op jit(solution)/shard_map/exchange/pallas_call | solution.py:575
  66.4 0.0 copy-done.4
  66.4 0.0 copy-done.1
  66.4 0.0 copy-done.2
  66.5 0.0 copy-done.3
  66.5 0.0 copy-done.6
  66.5 0.0 copy-done.5
  66.5 8.8 %derive.1 = (f32[48,128,256]{2,1,0:T(8,128)}, f32[48,128,256]{2,1,0:T(8,128)}) custom-call(f32[48,128,256]{2,1,0:T(8,128)S(1)} %bitcast.11, f32[2,384,128]{2,1,0:T(8,128)S(1)} %get-tuple-element.14.xh_ref, f32[384,128]{1,0:T(8,128)S(1)} %get-tuple-element.15.yh_ref, f32[16,128]{1,0:T(8,128)S(1)} %bitcast.14, f32[16,128]{1,0:T(8,128)S(1)} %bitcast.16, ...), custom_call_target="tpu_custom_call" | custom-call | bytes 31457280 | tf_op jit(solution)/shard_map/derive/pallas_call | solution.py:662
Async XLA Ops:
  0.6 65.8 %copy-start.4 = (bf16[32,512]{1,0:T(8,128)(2,1)S(1)}, bf16[32,512]{1,0:T(8,128)(2,1)}, u32[]{:S(2)}) copy-start(bf16[32,512]{1,0:T(8,128)(2,1)} %constant.11.clone.rim_ref) | copy-start | bytes 98308
  0.6 65.8 %copy-start.1 = (bf16[256,256]{1,0:T(8,128)(2,1)S(1)}, bf16[256,256]{1,0:T(8,128)(2,1)}, u32[]{:S(2)}) copy-start(bf16[256,256]{1,0:T(8,128)(2,1)} %constant.10.clone.kl_ref) | copy-start | bytes 393220
  0.7 65.8 %copy-start.2 = (bf16[256,256]{1,0:T(8,128)(2,1)S(1)}, bf16[256,256]{1,0:T(8,128)(2,1)}, u32[]{:S(2)}) copy-start(bf16[256,256]{1,0:T(8,128)(2,1)} %constant.9.clone.ky_ref) | copy-start | bytes 393220
  0.7 65.8 %copy-start.3 = (bf16[256,144]{1,0:T(8,128)(2,1)S(1)}, bf16[256,144]{1,0:T(8,128)(2,1)}, u32[]{:S(2)}) copy-start(bf16[256,144]{1,0:T(8,128)(2,1)} %constant.8.clone.kx_ref) | copy-start | bytes 221188
  0.7 65.8 %copy-start.6 = (f32[2048]{0:T(1024)S(1)}, f32[2048]{0:T(1024)}, u32[]{:S(2)}) copy-start(f32[2048]{0:T(1024)} %param.15) | copy-start | bytes 24580
  0.7 65.8 %copy-start.5 = (f32[2048]{0:T(1024)S(1)}, f32[2048]{0:T(1024)}, u32[]{:S(2)}) copy-start(f32[2048]{0:T(1024)} %param.14) | copy-start | bytes 24580
  20.8 0.9 %copy-start = (f32[18,8,1,256]{3,2,1,0:T(1,128)S(1)}, f32[18,8,1,256]{3,2,1,0:T(1,128)}, u32[]{:S(2)}) copy-start(f32[18,8,1,256]{3,2,1,0:T(1,128)} %shuffle.1) | copy-start | bytes 442372

commit v6 on v5

--- a/solution.py
+++ b/solution.py
@@ -412,7 +412,12 @@
         pltpu.make_async_copy(vbuf.at[:, z], e_hbm.at[:, z], e_sems.at[z]).start()
         return carry
 
-    lax.fori_loop(0, 16, plane, 0)
+    def some_planes(i, carry):
+        for j in range(4):
+            carry = plane(4 * i + j, carry)
+        return carry
+
+    lax.fori_loop(0, 4, some_planes, 0)
 
     corner = jnp.zeros((48, 128), F32)
     kinds = jnp.minimum(lax.broadcasted_iota(jnp.int32, (384, 128), 1), 7)
@@ -466,7 +471,7 @@
             pltpu.SemaphoreType.DMA((16,)),
             pltpu.SemaphoreType.DMA,
         ],
-        compiler_params=pltpu.CompilerParams(vmem_limit_bytes=45 << 20),
+        compiler_params=pltpu.CompilerParams(vmem_limit_bytes=47616 << 10),
         cost_estimate=cost(100 << 20),
         name="spread",
     )(inbox, v)

time: 75.4 us -> 75.4 us (level)
  no operation moved by 1% of the time
where the time goes in v6:
time: 75.4 us; the launch traced here: 75.3 us
  Pallas kernels  73.6 us (98%)
  local copies, waits for them, and re-layouts  0.94 us (1%)
  between operations  0.76 us (1%)
    pallas_call x1, Pallas kernels, spread(): pl.pallas_call(spread_kernel, out_shape=(jax.ShapeDtypeStruct(v.shape, F3...  32.6 us
    pallas_call x1, Pallas kernels, shuffle(): pl.pallas_call(shuffle_kernel, out_shape=jax.ShapeDtypeStruct((nx + 2, ny...  17 us
    pallas_call x1, Pallas kernels, exchange(): pl.pallas_call(exchange_kernel, out_shape=(jax.ShapeDtypeStruct((2, 8 * n...  12.2 us
    pallas_call x1, Pallas kernels, derive(): pl.pallas_call(derive_kernel, grid=(n // each,), out_shape=(jax.ShapeDtyp...  8.76 us
    pallas_call x1, Pallas kernels, pack(): pl.pallas_call(pack_kernel, out_shape=jax.ShapeDtypeStruct((8, counts.sha...  3.05 us

profile of v6, /device:TPU:1, one launch (start us, length us, event | category | flops | bytes accessed | tf_op | source)
XLA Modules:
  0.0 75.3 jit_solution(9709329225853868315)
XLA Ops:
  0.6 0.0 copy-start.4
  0.6 0.0 copy-start.1
  0.7 0.0 copy-start.2
  0.7 0.0 copy-start.3
  0.7 0.0 copy-start.6
  0.7 0.0 copy-start.5
  0.7 3.1 %pack.1.out_ref = f32[8,16,1,256]{3,2,1,0:T(1,128)} custom-call(s32[1,128]{1,0:T(1,128)} %counts_ref.1, f32[3,2048]{1,0:T(4,128)} %force_ref.1, f32[3,2048]{1,0:T(4,128)} %frac_ref.1, s32[16,128]{1,0:T(8,128)} %bitcast.17, s32[16,128]{1,0:T(8,128)} %bitcast.18, s32[16,128]{1,0:T(8,128)} %bitcast.19), custom_call_target="tpu_custom_call" | custom-call | bytes 12582912 | tf_op jit(solution)/shard_map/pack/pallas_call | solution.py:115
  3.8 17.0 %shuffle.1 = f32[18,8,1,256]{3,2,1,0:T(1,128)} custom-call(f32[8,16,1,256]{3,2,1,0:T(1,128)} %pack.1.out_ref, f32[8,1,256]{2,1,0:T(1,128)} %bitcast.13, f32[8,1,256]{2,1,0:T(1,128)} %bitcast.15), custom_call_target="tpu_custom_call" | custom-call | bytes 37748736 | tf_op jit(solution)/shard_map/shuffle/pallas_call | solution.py:174
  20.8 0.0 copy-start
  20.8 0.9 %copy-done = f32[18,8,1,256]{3,2,1,0:T(1,128)S(1)} copy-done((f32[18,8,1,256]{3,2,1,0:T(1,128)S(1)}, f32[18,8,1,256]{3,2,1,0:T(1,128)}, u32[]{:S(2)}) %copy-start) | copy-done | bytes 147480
  21.7 32.6 %spread.1 = (f32[3,16,128,256]{3,2,1,0:T(8,128)S(1)}, f32[8,48,256]{2,1,0:T(8,128)S(1)}, f32[48,128]{1,0:T(8,128)S(1)}, f32[8,48,128]{2,1,0:T(8,128)S(1)}) custom-call(f32[144,1,256]{2,1,0:T(1,128)S(1)} %bitcast.12, f32[3,16,128,256]{3,2,1,0:T(8,128)} %v_hbm.1), custom_call_target="tpu_custom_call" | custom-call | bytes 104857600 | tf_op jit(solution)/shard_map/spread/pallas_call | solution.py:447
  54.2 12.2 %exchange.1 = (f32[2,384,128]{2,1,0:T(8,128)S(1)}, f32[384,128]{1,0:T(8,128)S(1)}) custom-call(f32[8,48,256]{2,1,0:T(8,128)S(1)} %get-tuple-element.11.rl_hbm, f32[48,128]{1,0:T(8,128)S(1)} %get-tuple-element.12.cn_hbm, f32[8,48,128]{2,1,0:T(8,128)S(1)} %get-tuple-element.13.ud_hbm), custom_call_target="tpu_custom_call" | custom-call | bytes 31457280 | tf_op jit(solution)/shard_map/exchange/pallas_call | solution.py:580
  66.5 0.0 copy-done.4
  66.5 0.0 copy-done.1
  66.5 0.0 copy-done.2
  66.5 0.0 copy-done.3
  66.5 0.0 copy-done.6
  66.5 0.0 copy-done.5
  66.6 8.8 %derive.1 = (f32[48,128,256]{2,1,0:T(8,128)}, f32[48,128,256]{2,1,0:T(8,128)}) custom-call(f32[48,128,256]{2,1,0:T(8,128)S(1)} %bitcast.11, f32[2,384,128]{2,1,0:T(8,128)S(1)} %get-tuple-element.14.xh_ref, f32[384,128]{1,0:T(8,128)S(1)} %get-tuple-element.15.yh_ref, f32[16,128]{1,0:T(8,128)S(1)} %bitcast.14, f32[16,128]{1,0:T(8,128)S(1)} %bitcast.16, ...), custom_call_target="tpu_custom_call" | custom-call | bytes 31457280 | tf_op jit(solution)/shard_map/derive/pallas_call | solution.py:667
Async XLA Ops:
  0.6 65.9 %copy-start.4 = (bf16[32,512]{1,0:T(8,128)(2,1)S(1)}, bf16[32,512]{1,0:T(8,128)(2,1)}, u32[]{:S(2)}) copy-start(bf16[32,512]{1,0:T(8,128)(2,1)} %constant.11.clone.rim_ref) | copy-start | bytes 98308
  0.6 65.9 %copy-start.1 = (bf16[256,256]{1,0:T(8,128)(2,1)S(1)}, bf16[256,256]{1,0:T(8,128)(2,1)}, u32[]{:S(2)}) copy-start(bf16[256,256]{1,0:T(8,128)(2,1)} %constant.10.clone.kl_ref) | copy-start | bytes 393220
  0.7 65.9 %copy-start.2 = (bf16[256,256]{1,0:T(8,128)(2,1)S(1)}, bf16[256,256]{1,0:T(8,128)(2,1)}, u32[]{:S(2)}) copy-start(bf16[256,256]{1,0:T(8,128)(2,1)} %constant.9.clone.ky_ref) | copy-start | bytes 393220
  0.7 65.9 %copy-start.3 = (bf16[256,144]{1,0:T(8,128)(2,1)S(1)}, bf16[256,144]{1,0:T(8,128)(2,1)}, u32[]{:S(2)}) copy-start(bf16[256,144]{1,0:T(8,128)(2,1)} %constant.8.clone.kx_ref) | copy-start | bytes 221188
  0.7 65.9 %copy-start.6 = (f32[2048]{0:T(1024)S(1)}, f32[2048]{0:T(1024)}, u32[]{:S(2)}) copy-start(f32[2048]{0:T(1024)} %param.15) | copy-start | bytes 24580
  0.7 65.9 %copy-start.5 = (f32[2048]{0:T(1024)S(1)}, f32[2048]{0:T(1024)}, u32[]{:S(2)}) copy-start(f32[2048]{0:T(1024)} %param.14) | copy-start | bytes 24580
  20.8 0.9 %copy-start = (f32[18,8,1,256]{3,2,1,0:T(1,128)S(1)}, f32[18,8,1,256]{3,2,1,0:T(1,128)}, u32[]{:S(2)}) copy-start(f32[18,8,1,256]{3,2,1,0:T(1,128)} %shuffle.1) | copy-start | bytes 442372
